TPU v7x, 256 devices: a whole 4x4x8 slice. The times are simulated.
256 devices in a mesh: freq: 8 (over x, core), tile: 32 (over y, z).
Axes of the slice: x: 4, y: 4, z: 8, core: 2. Of those that a mesh axis runs over, the one named last changes fastest.
Arguments:
- model_field: bfloat16 [8, 16384, 256], P('freq', 'tile'), may hold values from -6 to 6
- data_field: bfloat16 [8, 16384, 256], P('freq', 'tile'), may hold values from -6 to 6
- u_codes: bfloat16 [8, 2, 16384, 2816], P('freq', None, 'tile'), may hold values from -128 to 127, as said below
- u_scales: float32 [8, 32, 2816], P('freq', 'tile'), as said below
- v_codes: bfloat16 [8, 2, 16384, 2816], P('freq', None, 'tile'), may hold values from -128 to 127, as said below
- v_scales: float32 [8, 32, 2816], P('freq', 'tile'), as said below
- tile_ranks: int32 [8, 32, 32], P('freq'), may hold values from 40 to 88, as said below
- mute_start: int32 [16384], P('tile'), may hold values from 0 to 64
Outputs:
- gradient_time: bfloat16 [16384, 128, 128], P('tile', 'freq')
Inputs may be any that keep to these rules, and one draw needn't show every extreme that they name: `tile_ranks`: for every frequency the ranks are symmetric; one tile row (and column), drawn per frequency, has every tile of rank 88, so its total is exactly 2816; no row or column totals more. `u_codes`: whole numbers. `v_codes`: whole numbers. `u_scales`: Positive. `v_scales`: Positive.
All inputs are finite; a program needn't handle non-finite values.
Results may differ from a plain program's by a relative error of at most 0.0075.
Values may be sent and summed in bfloat16 or wider, within the bound.
No kernel may reach another device: no remote copies, remote signals or barrier semaphores. Data moves between devices by JAX's collectives and lax.ppermute only.
A program may use at most 128 MiB of HBM per device.

v0:
```python
import math

import jax
import jax.numpy as jnp
from jax import lax
from jax.sharding import PartitionSpec as P

RSLOT = 88
NTIME = 128


def unpack_pool(code_vals, scale_row):
    return (code_vals.astype(jnp.float32) * scale_row).astype(jnp.bfloat16)


def apply_factor(factor, pooled):
    half_width = pooled.shape[1] // 2
    real_part = jnp.dot(factor[0], pooled, preferred_element_type=jnp.float32)
    imag_part = jnp.dot(factor[1], pooled, preferred_element_type=jnp.float32)
    out_re = real_part[:, :half_width] - imag_part[:, half_width:]
    out_im = real_part[:, half_width:] + imag_part[:, :half_width]
    return jnp.concatenate([out_re, out_im], 1)


def apply_adjoint(factor, dense_rows):
    half_width = dense_rows.shape[1] // 2
    dims = (((0,), (0,)), ((), ()))
    real_part = lax.dot_general(factor[0], dense_rows, dims, preferred_element_type=jnp.float32)
    imag_part = lax.dot_general(factor[1], dense_rows, dims, preferred_element_type=jnp.float32)
    out_re = real_part[:, :half_width] + imag_part[:, half_width:]
    out_im = real_part[:, half_width:] - imag_part[:, :half_width]
    return jnp.concatenate([out_re, out_im], 1)


def pool_owner(ends, begins, capacity, tile_count):
    column = jnp.arange(capacity, dtype=jnp.int32)
    owner_raw = jnp.sum((column[:, None] >= ends[None, :]).astype(jnp.int32), 1)
    is_live = owner_raw < tile_count
    owner_tile = jnp.minimum(owner_raw, tile_count - 1)
    offset = column - begins[owner_tile]
    return (owner_tile, offset, is_live)


def fill_slots(pooled, begins, rank_vec):
    slot_pos = jnp.arange(RSLOT, dtype=jnp.int32)
    is_live = slot_pos[None, :] < rank_vec[:, None]
    source = jnp.where(is_live, begins[:, None] + slot_pos[None, :], 0)
    picked = pooled[source.reshape(-1)].reshape(rank_vec.shape[0], RSLOT, pooled.shape[1])
    return jnp.where(is_live[:, :, None], picked, 0)


def pool_from_slots(arrived, ends, begins, capacity):
    tile_count = arrived.shape[0]
    flat_slots = arrived.reshape(tile_count * RSLOT, arrived.shape[2])
    owner_tile, offset, is_live = pool_owner(ends, begins, capacity, tile_count)
    source = jnp.where(is_live, owner_tile * RSLOT + offset, 0)
    return jnp.where(is_live[:, None], flat_slots[source], 0)


def shards(model_field, data_field, u_codes, u_scales, v_codes, v_scales, tile_ranks, mute_start):
    my_tile = lax.axis_index("tile")
    rank_table = tile_ranks[0]
    row_ranks = rank_table[my_tile]
    col_ranks = rank_table[:, my_tile]
    row_end = jnp.cumsum(row_ranks)
    row_begin = row_end - row_ranks
    col_end = jnp.cumsum(col_ranks)
    col_begin = col_end - col_ranks
    v_factor = unpack_pool(v_codes[0], v_scales[0, 0])
    u_factor = unpack_pool(u_codes[0], u_scales[0, 0])
    capacity = v_factor.shape[2]
    rows_here = model_field.shape[1]
    sources = model_field.shape[2] // 2
    w_pool = apply_adjoint(v_factor, model_field[0]).astype(jnp.bfloat16)
    w_slots = fill_slots(w_pool, col_begin, col_ranks)
    w_arrived = lax.all_to_all(w_slots, "tile", split_axis=0, concat_axis=0, tiled=True)
    w_rows = pool_from_slots(w_arrived, row_end, row_begin, capacity)
    predicted = apply_factor(u_factor, w_rows)
    residual = (predicted - data_field[0].astype(jnp.float32)).astype(jnp.bfloat16)
    p_pool = apply_adjoint(u_factor, residual).astype(jnp.bfloat16)
    p_slots = fill_slots(p_pool, row_begin, row_ranks)
    p_arrived = lax.all_to_all(p_slots, "tile", split_axis=0, concat_axis=0, tiled=True)
    p_cols = pool_from_slots(p_arrived, col_end, col_begin, capacity)
    gradient = apply_factor(v_factor, p_cols).astype(jnp.bfloat16)
    freq_count = lax.axis_size("freq")
    share = sources // freq_count
    sectioned = gradient.reshape(1, rows_here, 2, freq_count, share)
    arrived = lax.all_to_all(sectioned, "freq", split_axis=3, concat_axis=0, tiled=True)
    spectra = arrived.reshape(freq_count, rows_here, 2, share).astype(jnp.float32)
    freq_bin = jnp.arange(freq_count, dtype=jnp.int32).astype(jnp.float32) + 1.0
    time_grid = jnp.arange(NTIME, dtype=jnp.int32).astype(jnp.float32)
    phase_arg = 2.0 * math.pi * freq_bin[:, None] * time_grid[None, :] / NTIME
    time_basis = jnp.stack([jnp.cos(phase_arg), -jnp.sin(phase_arg)], 1)
    signal = 0.5 * jnp.einsum("fncs,fct->nst", spectra, time_basis, precision=lax.Precision.HIGHEST)
    unmuted = jnp.arange(NTIME, dtype=jnp.int32)[None, None, :] >= mute_start[:, None, None]
    return jnp.where(unmuted, signal, 0.0).astype(jnp.bfloat16)


def solution(mesh):
    in_specs = (
        P("freq", "tile", None),
        P("freq", "tile", None),
        P("freq", None, "tile", None),
        P("freq", "tile", None),
        P("freq", None, "tile", None),
        P("freq", "tile", None),
        P("freq", None, None),
        P("tile"),
    )
    out_specs = P("tile", "freq", None)
    return jax.shard_map(shards, mesh=mesh, in_specs=in_specs, out_specs=out_specs, check_vma=False)
```

profile of v0, /device:TPU:1, one launch (start us, length us, event | category | flops | bytes accessed | tf_op | source)
XLA Modules:
  0.0 171.7 jit_solution(5942301134662175758)
XLA Ops:
  0.8 3.7 %fusion.1 = bf16[2,512,2816]{2,1,0:T(8,128)(2,1)S(1)} fusion(bf16[1,2,512,2816]{3,2,1,0:T(8,128)(2,1)} %param.12, f32[2816]{0:T(1024)S(1)} %reduce), kind=kLoop, calls=%fused_computation.7 | loop fusion | flops 8650752 | bytes 11545600 | tf_op jit(solution)/shard_map/convert_element_type | solution.py:13
  5.5 1.5 copy-done.1
  7.0 2.5 %fusion.9 = f32[2816,256]{0,1:T(8,128)} fusion(bf16[2,512,2816]{2,1,0:T(8,128)(2,1)S(1)} %fusion.1, bf16[1,512,256]{2,1,0:T(8,128)(2,1)S(1)} %copy-done), kind=kOutput, calls=%fused_computation.20 | convolution fusion | flops 738197504 | bytes 6029312 | tf_op jit(solution)/shard_map/dot_general | solution.py:29
  10.2 2.1 %fusion.15 = (bf16[2816,128]{0,1:T(8,128)(2,1)S(1)}, bf16[2816,128]{0,1:T(8,128)(2,1)S(1)}) fusion(f32[2816,256]{0,1:T(8,128)} %fusion.9, f32[2816,256]{0,1:T(8,128)S(1)} %fusion.5), kind=kLoop, calls=%fused_computation.30 | loop fusion | flops 1441792 | bytes 7208960 | tf_op jit(solution)/shard_map/convert.6
  13.1 8.3 %gather_fusion = bf16[2816,256]{1,0:T(8,128)(2,1)S(1)} fusion(bf16[2816,256]{1,0:T(8,128)(2,1)S(1)} %copy.33, s32[3072]{0:T(1024)S(1)} %pad_clamp_fusion.3), kind=kCustom, calls=%fused_computation | custom fusion | bytes 2894848 | tf_op jit(solution)/shard_map/gather | solution.py:48
  22.7 12.3 %all-to-all-start = ((bf16[32,88,256]{2,1,0:T(8,128)(2,1)}), bf16[32,88,256]{2,1,0:T(8,128)(2,1)S(1)}, u32[]{:S(2)}, u32[]{:S(2)}) async-start(bf16[32,88,256]{2,1,0:T(8,128)(2,1)} %broadcast_select_fusion.2), calls=%async_computation | async-start | bytes 2883584 | tf_op jit(solution)/shard_map/all_to_all | solution.py:76
  36.6 4.5 %fusion.26 = (s32[2816]{0:T(1024)S(1)}, s32[2816,1]{0,1:T(1,128)S(1)}) fusion(s32[]{:T(128)} %bitcast.36, s32[]{:T(128)} %bitcast.37, s32[]{:T(128)} %bitcast.38, s32[]{:T(128)} %bitcast.39, s32[]{:T(128)} %bitcast.40, s32[]{:T(128)} %bitcast.42, s32[]{:T(128)} %bitcast.41, s32[2816]{0:T(1024)S(1)} %broadcast_minimum_fusion.1), kind=kLoop, calls=%fused_computation.140 | loop fusion | flops 42240 | bytes 33820 | tf_op jit(solution)/shard_map/gather | solution.py:40
  42.7 15.5 %select_select_fusion.1 = s32[2816]{0:T(1024)S(1)} fusion(pred[2816]{0:T(1024)(128)(4,1)S(1)} %get-tuple-element.54, pred[2816]{0:T(1024)(128)(4,1)S(1)} %get-tuple-element.53, pred[2816]{0:T(1024)(128)(4,1)S(1)} %get-tuple-element.52, pred[2816]{0:T(1024)(128)(4,1)S(1)} %get-tuple-element.51, pred[2816]{0:T(1024)(128)(4,1)S(1)} %get-tuple-element.50, ...), kind=kLoop, calls=%fused_computation.139 | loop fusion | flops 70400 | bytes 93028 | tf_op jit(solution)/shard_map/gather | solution.py:40
  58.5 6.2 %fusion = bf16[2,512,2816]{2,1,0:T(8,128)(2,1)} fusion(bf16[1,2,512,2816]{3,2,1,0:T(8,128)(2,1)} %param.10, f32[2816]{0:T(1024)S(1)} %reduce.2), kind=kLoop, calls=%fused_computation.5 | loop fusion | flops 8650752 | bytes 11545600 | tf_op jit(solution)/shard_map/convert_element_type | solution.py:13
  64.7 4.3 %all-to-all-done = bf16[32,88,256]{2,1,0:T(8,128)(2,1)S(1)} async-done(((bf16[32,88,256]{2,1,0:T(8,128)(2,1)}), bf16[32,88,256]{2,1,0:T(8,128)(2,1)S(1)}, u32[]{:S(2)}, u32[]{:S(2)}) %all-to-all-start) | async-done | bytes 1441824 | tf_op jit(solution)/shard_map/all_to_all | solution.py:76
  69.0 8.3 %gather_fusion.1 = bf16[2816,256]{1,0:T(8,128)(2,1)S(1)} fusion(bf16[2816,256]{1,0:T(8,128)(2,1)S(1)} %bitcast.128, s32[3072]{0:T(1024)S(1)} %pad_clamp_fusion.2), kind=kCustom, calls=%fused_computation.1 | custom fusion | bytes 2894848 | tf_op jit(solution)/shard_map/gather | solution.py:57
  77.2 3.2 %fusion.7 = f32[512,256]{0,1:T(8,128)S(1)} fusion(bf16[2,512,2816]{2,1,0:T(8,128)(2,1)} %fusion, bf16[2816,256]{1,0:T(8,128)(2,1)S(1)} %gather_fusion.1, pred[2816]{0:T(1024)(128)(4,1)S(1)} %broadcast_compare_fusion), kind=kOutput, calls=%fused_computation.18 | convolution fusion | flops 738918400 | bytes 4852480 | tf_op jit(solution)/shard_map/dot_general | solution.py:18
  85.1 8.3 %gather_fusion.2 = bf16[2816,256]{1,0:T(8,128)(2,1)S(1)} fusion(bf16[2816,256]{1,0:T(8,128)(2,1)S(1)} %copy.35, s32[3072]{0:T(1024)S(1)} %pad_clamp_fusion.1), kind=kCustom, calls=%fused_computation.2 | custom fusion | bytes 2894848 | tf_op jit(solution)/shard_map/gather | solution.py:48
  94.8 7.8 %all-to-all-start.1 = ((bf16[32,88,256]{2,1,0:T(8,128)(2,1)}), bf16[32,88,256]{2,1,0:T(8,128)(2,1)S(1)}, u32[]{:S(2)}, u32[]{:S(2)}) async-start(bf16[32,88,256]{2,1,0:T(8,128)(2,1)} %broadcast_select_fusion.3), calls=%async_computation.1 | async-start | bytes 2883584 | tf_op jit(solution)/shard_map/all_to_all | solution.py:82
  103.5 4.5 %fusion.27 = (s32[2816]{0:T(1024)S(1)}, s32[2816,1]{0,1:T(1,128)S(1)}) fusion(s32[]{:T(128)} %bitcast.74, s32[]{:T(128)} %bitcast.75, s32[]{:T(128)} %bitcast.76, s32[]{:T(128)} %bitcast.77, s32[]{:T(128)} %bitcast.78, s32[]{:T(128)} %bitcast.80, s32[]{:T(128)} %bitcast.79, s32[2816]{0:T(1024)S(1)} %broadcast_minimum_fusion), kind=kLoop, calls=%fused_computation.141 | loop fusion | flops 42240 | bytes 33820 | tf_op jit(solution)/shard_map/gather | solution.py:40
  109.5 15.5 %select_select_fusion = s32[2816]{0:T(1024)S(1)} fusion(pred[2816]{0:T(1024)(128)(4,1)S(1)} %get-tuple-element.29, pred[2816]{0:T(1024)(128)(4,1)S(1)} %get-tuple-element.28, pred[2816]{0:T(1024)(128)(4,1)S(1)} %get-tuple-element.27, pred[2816]{0:T(1024)(128)(4,1)S(1)} %get-tuple-element.26, pred[2816]{0:T(1024)(128)(4,1)S(1)} %get-tuple-element.25, ...), kind=kLoop, calls=%fused_computation.138 | loop fusion | flops 70400 | bytes 93028 | tf_op jit(solution)/shard_map/gather | solution.py:40
  125.2 11.4 %all-to-all-done.1 = bf16[32,88,256]{2,1,0:T(8,128)(2,1)S(1)} async-done(((bf16[32,88,256]{2,1,0:T(8,128)(2,1)}), bf16[32,88,256]{2,1,0:T(8,128)(2,1)S(1)}, u32[]{:S(2)}, u32[]{:S(2)}) %all-to-all-start.1) | async-done | bytes 1441824 | tf_op jit(solution)/shard_map/all_to_all | solution.py:82
  136.6 8.3 %gather_fusion.3 = bf16[2816,256]{1,0:T(8,128)(2,1)S(1)} fusion(bf16[2816,256]{1,0:T(8,128)(2,1)S(1)} %bitcast.129, s32[3072]{0:T(1024)S(1)} %pad_clamp_fusion), kind=kCustom, calls=%fused_computation.3 | custom fusion | bytes 2894848 | tf_op jit(solution)/shard_map/gather | solution.py:57
  144.8 3.1 %fusion.4 = f32[512,256]{0,1:T(8,128)S(1)} fusion(bf16[2,512,2816]{2,1,0:T(8,128)(2,1)} %copy-done.1, bf16[2816,256]{1,0:T(8,128)(2,1)S(1)} %gather_fusion.3, pred[2816]{0:T(1024)(128)(4,1)S(1)} %broadcast_compare_fusion.1), kind=kOutput, calls=%fused_computation.15 | convolution fusion | flops 738918400 | bytes 4852480 | tf_op jit(solution)/shard_map/dot_general | solution.py:18
  147.9 3.1 %fusion.8 = f32[512,256]{0,1:T(8,128)S(1)} fusion(bf16[2,512,2816]{2,1,0:T(8,128)(2,1)} %copy-done.1, bf16[2816,256]{1,0:T(8,128)(2,1)S(1)} %gather_fusion.3, pred[2816]{0:T(1024)(128)(4,1)S(1)} %broadcast_compare_fusion.1), kind=kOutput, calls=%fused_computation.19 | convolution fusion | flops 738918400 | bytes 4852480 | tf_op jit(solution)/shard_map/dot_general | solution.py:19
  152.2 7.8 %all-to-all-start.2 = ((bf16[1,512,2,8,16]{1,2,4,0,3:T(2,128)(2,1)}), bf16[1,512,2,8,16]{1,2,4,0,3:T(2,128)(2,1)S(1)}, u32[]{:S(2)}, u32[]{:S(2)}) async-start(bf16[1,512,2,8,16]{1,2,4,0,3:T(2,128)(2,1)} %copy.36), calls=%async_computation.2 | async-start | bytes 524288 | tf_op jit(solution)/shard_map/all_to_all | solution.py:88
  160.3 6.2 %all-to-all-done.2 = bf16[1,512,2,8,16]{1,2,4,0,3:T(2,128)(2,1)S(1)} async-done(((bf16[1,512,2,8,16]{1,2,4,0,3:T(2,128)(2,1)}), bf16[1,512,2,8,16]{1,2,4,0,3:T(2,128)(2,1)S(1)}, u32[]{:S(2)}, u32[]{:S(2)}) %all-to-all-start.2) | async-done | bytes 262176 | tf_op jit(solution)/shard_map/all_to_all | solution.py:88
  166.5 2.5 %fusion.3 = bf16[512,16,128]{2,0,1:T(8,128)(2,1)S(1)} fusion(pred[512,128]{1,0:T(8,128)(4,1)S(1)} %iota_compare_fusion.2, bf16[1,512,2,8,16]{1,2,4,0,3:T(2,128)(2,1)S(1)} %all-to-all-done.2, f32[8,1,128]{2,0,1:T(8,128)S(1)} %get-tuple-element.72, f32[8,1,128]{2,0,1:T(8,128)S(1)} %get-tuple-element.71), kind=kOutput, calls=%fused_computation.10 | convolution fusion | flops 204474368 | bytes 2433024 | tf_op jit(solution)/shard_map/fncs,fct->nst/dot_general | solution.py:94
  169.0 2.7 %copy.38 = bf16[512,16,128]{2,1,0:T(8,128)(2,1)} copy(bf16[512,16,128]{2,0,1:T(8,128)(2,1)S(1)} %fusion.3) | data formatting | bytes 4194304 | tf_op jit(solution)/shard_map/convert_element_type | solution.py:96
  (70 shorter events, 17.7 us)
Async XLA Ops:
  0.0 4.5 %copy-start = (bf16[1,512,256]{2,1,0:T(8,128)(2,1)S(1)}, bf16[1,512,256]{2,1,0:T(8,128)(2,1)}, u32[]{:S(2)}) copy-start(bf16[1,512,256]{2,1,0:T(8,128)(2,1)} %param.8) | copy-start | bytes 786436
  4.5 2.5 %copy-start.1 = (bf16[2,512,2816]{2,1,0:T(8,128)(2,1)}, bf16[2,512,2816]{2,1,0:T(8,128)(2,1)S(1)}, u32[]{:S(2)}) copy-start(bf16[2,512,2816]{2,1,0:T(8,128)(2,1)S(1)} %fusion.1) | copy-start | bytes 17301508
  7.0 2.5 %copy-start.4 = (s32[1,32,32]{2,1,0:T(8,128)S(1)}, s32[1,32,32]{2,1,0:T(8,128)}, u32[]{:S(2)}) copy-start(s32[1,32,32]{2,1,0:T(8,128)} %param.14) | copy-start | bytes 12292
  22.7 12.6 %copy-start.5 = (f32[1,1,2816]{2,1,0:T(1,128)S(1)}, f32[1,1,2816]{2,1,0:T(1,128)}, u32[]{:S(2)}) copy-start(f32[1,1,2816]{2,1,0:T(1,128)} %param.11) | copy-start | bytes 33796
  22.7 12.7 %copy-start.3 = (bf16[1,512,256]{2,1,0:T(8,128)(2,1)S(1)}, bf16[1,512,256]{2,1,0:T(8,128)(2,1)}, u32[]{:S(2)}) copy-start(bf16[1,512,256]{2,1,0:T(8,128)(2,1)} %param.9) | copy-start | bytes 786436
  22.7 46.2 %all-to-all-start = ((bf16[32,88,256]{2,1,0:T(8,128)(2,1)}), bf16[32,88,256]{2,1,0:T(8,128)(2,1)S(1)}, u32[]{:S(2)}, u32[]{:S(2)}) async-start(bf16[32,88,256]{2,1,0:T(8,128)(2,1)} %broadcast_select_fusion.2), calls=%async_computation | async-start | bytes 2883584 | tf_op jit(solution)/shard_map/all_to_all | solution.py:76
  77.2 3.5 %copy-start.2 = (bf16[2,512,2816]{2,1,0:T(8,128)(2,1)S(1)}, bf16[2,512,2816]{2,1,0:T(8,128)(2,1)}, u32[]{:S(2)}) copy-start(bf16[2,512,2816]{2,1,0:T(8,128)(2,1)} %fusion) | copy-start | bytes 17301508
  94.8 41.8 %all-to-all-start.1 = ((bf16[32,88,256]{2,1,0:T(8,128)(2,1)}), bf16[32,88,256]{2,1,0:T(8,128)(2,1)S(1)}, u32[]{:S(2)}, u32[]{:S(2)}) async-start(bf16[32,88,256]{2,1,0:T(8,128)(2,1)} %broadcast_select_fusion.3), calls=%async_computation.1 | async-start | bytes 2883584 | tf_op jit(solution)/shard_map/all_to_all | solution.py:82
  151.0 9.1 %copy-start.6 = (s32[512]{0:T(512)S(1)}, s32[512]{0:T(512)}, u32[]{:S(2)}) copy-start(s32[512]{0:T(512)} %param.15) | copy-start | bytes 6148
  152.2 14.3 %all-to-all-start.2 = ((bf16[1,512,2,8,16]{1,2,4,0,3:T(2,128)(2,1)}), bf16[1,512,2,8,16]{1,2,4,0,3:T(2,128)(2,1)S(1)}, u32[]{:S(2)}, u32[]{:S(2)}) async-start(bf16[1,512,2,8,16]{1,2,4,0,3:T(2,128)(2,1)} %copy.36), calls=%async_computation.2 | async-start | bytes 524288 | tf_op jit(solution)/shard_map/all_to_all | solution.py:88
where the time goes:
time: 173 us; the launch traced here: 172 us
  other arithmetic  59.4 us (34%)
  local copies, waits for them, and re-layouts  43.4 us (25%)
  starting transfers between devices  28 us (16%)
  waiting for transfers between devices  21.9 us (13%)
  matrix products  18.6 us (11%)
    gather x6, other arithmetic, pool_owner(): offset = column - begins[owner_tile]  41.7 us
    gather x2, local copies, waits for them, and re-layouts, fill_slots(): pooled[source.reshape(-1)]  16.5 us
    gather x2, local copies, waits for them, and re-layouts, pool_from_slots(): return jnp.where(is_live[:, None], flat_slots[source], 0)  16.5 us
    all_to_all x1, starting transfers between devices, shards(): lax.all_to_all(w_slots, 'tile', split_axis=0, concat_axis=0, tiled=True)  12.3 us
    all_to_all x1, waiting for transfers between devices, shards(): lax.all_to_all(p_slots, 'tile', split_axis=0, concat_axis=0, tiled=True)  11.4 us
    convert_element_type x2, other arithmetic, unpack_pool(): return (code_vals.astype(jnp.float32) * scale_row).astype(jnp.bfloat16)  9.92 us
    all_to_all x1, starting transfers between devices, shards(): lax.all_to_all(sectioned, 'freq', split_axis=3, concat_axis=0, tiled=True)  7.83 us
    all_to_all x1, starting transfers between devices, shards(): lax.all_to_all(p_slots, 'tile', split_axis=0, concat_axis=0, tiled=True)  7.79 us
  transfers between devices with their start and end apart: 3, of which 3 were waited for; matrix products, arithmetic and copies ran while one was open for 30% of the time, Pallas kernels for 0%

commit v1 on v0

v1 whole, which is shorter than its diff:
```python
import functools
import math

import jax
import jax.numpy as jnp
import numpy as np
from jax import lax
from jax.experimental import pallas as pl
from jax.experimental.pallas import tpu as pltpu
from jax.sharding import PartitionSpec as P

RSLOT = 88
NTIME = 128
BLK = 256
WIN = 384
F32 = jnp.float32
BF16 = jnp.bfloat16
NT_DIMS = (((1,), (1,)), ((), ()))


def time_basis(freq_count, per):
    arg = 2.0 * math.pi * (np.arange(freq_count)[:, None] + 1.0) * np.arange(NTIME)[None, :] / NTIME
    base = 0.5 * np.stack([np.cos(arg), -np.sin(arg)], 1)
    rows = np.repeat(base.reshape(freq_count * 2, NTIME), per, 0).astype(np.float32)
    high = rows.astype(jnp.bfloat16)
    low = (rows - high.astype(np.float32)).astype(jnp.bfloat16)
    return np.concatenate([high, low], 1)


def start_all(*copies):
    for copy in copies:
        copy.start()
    return copies


def coef_kernel(ranks_in, codes, scale_in, model_in, out, ranks, scale, model, plain, rotated, held, first, pool, sems):
    parts, rows, cap = codes.shape
    tiles = ranks.shape[0]
    half = model.shape[1] // 2
    mine = lax.axis_index("tile")
    small = start_all(
        pltpu.make_async_copy(model_in, model, sems.at[0]),
        pltpu.make_async_copy(scale_in, scale, sems.at[1]),
        pltpu.make_async_copy(ranks_in, ranks, sems.at[2]),
    )
    big = start_all(*[pltpu.make_async_copy(codes.at[part], held.at[part], sems.at[3 + part]) for part in range(parts)])
    for lane in range(2):
        pool[lane, cap:cap + RSLOT + 8, :] = jnp.zeros((RSLOT + 8, 128), F32)
    small[0].wait()
    turned = model[...].astype(F32).T
    plain[...] = turned.astype(BF16)
    rotated[:half] = turned[half:].astype(BF16)
    rotated[half:] = (-turned[:half]).astype(BF16)
    small[1].wait()
    small[2].wait()
    piece = cap // 2
    big[0].wait()
    for at in range(0, cap, piece):
        first[:, at:at + piece] = jnp.dot(plain[...], held[0, :, at:at + piece], preferred_element_type=F32)
    big[1].wait()
    for at in range(0, cap, piece):
        acc = first[:, at:at + piece] + jnp.dot(rotated[...], held[1, :, at:at + piece], preferred_element_type=F32)
        upright = (acc * scale[:, at:at + piece]).T
        for lane in range(2):
            pool[lane, at:at + piece, :] = upright[:, lane * 128:lane * 128 + 128]

    def move(tile, begin):
        for lane in range(2):
            out[tile, :, lane * 128:lane * 128 + 128] = pool[lane, pl.ds(begin, RSLOT), :].astype(BF16)
        return begin + ranks[tile, mine]

    lax.fori_loop(0, tiles, move, jnp.int32(0))


def in_hbm(*arrays):
    return [pltpu.with_memory_space_constraint(array, pltpu.HBM) for array in arrays]


def coef(ranks, codes, scale, model):
    parts, rows, cap = codes.shape
    width = model.shape[1]
    tiles = ranks.shape[0]
    return pl.pallas_call(
        coef_kernel,
        in_specs=[pl.BlockSpec(memory_space=pl.ANY)] * 4,
        out_specs=pl.BlockSpec(memory_space=pltpu.VMEM),
        out_shape=jax.ShapeDtypeStruct((tiles, RSLOT, width), BF16),
        scratch_shapes=[
            pltpu.SMEM(ranks.shape, jnp.int32),
            pltpu.VMEM(scale.shape, F32),
            pltpu.VMEM(model.shape, BF16),
            pltpu.VMEM((width, rows), BF16),
            pltpu.VMEM((width, rows), BF16),
            pltpu.VMEM((parts, rows, cap), BF16),
            pltpu.VMEM((width, cap), F32),
            pltpu.VMEM((2, cap + RSLOT + 8, 128), F32),
            pltpu.SemaphoreType.DMA((3 + parts,)),
        ],
        compiler_params=pltpu.CompilerParams(vmem_limit_bytes=32 << 20),
        cost_estimate=pl.CostEstimate(flops=4 * cap * rows * width, bytes_accessed=parts * rows * cap * 2, transcendentals=0),
        name="coef",
    )(*in_hbm(ranks, codes, scale, model))


def slot_kernel(by_row, with_turned, ranks, codes, scale, *rest):
    out = rest[0]
    turned = rest[1] if with_turned else None
    begin, rank = rest[-2:]
    step = pl.program_id(0)
    tiles = ranks.shape[0]
    cap = codes.shape[2]
    mine = lax.axis_index("tile")

    @pl.when(step == 0)
    def _():
        def fill(tile, acc):
            here = ranks[mine, tile] if by_row else ranks[tile, mine]
            begin[tile] = acc
            rank[tile] = here
            return acc + here

        lax.fori_loop(0, tiles, fill, jnp.int32(0))

    first_tile = (step * BLK) // RSLOT
    inside = step * BLK - first_tile * RSLOT
    first = begin[first_tile] + jnp.minimum(inside, rank[first_tile])
    start = pl.multiple_of(jnp.minimum((first // 128) * 128, cap - WIN), 128)
    lane = lax.broadcasted_iota(jnp.int32, (1, BLK), 1)
    where_from = jnp.full((1, BLK), -1, jnp.int32)
    for ahead in range(-(-BLK // RSLOT) + 1):
        tile = jnp.minimum(first_tile + ahead, tiles - 1)
        offset = lane + (step * BLK - tile * RSLOT)
        live = (offset >= 0) & (offset < rank[tile])
        where_from = jnp.where(live, offset + (begin[tile] - start), where_from)
    picks = jnp.where(lax.broadcasted_iota(jnp.int32, (WIN, BLK), 0) == where_from, 1.0, 0.0).astype(BF16)
    window = scale[:, pl.ds(start, WIN)]
    high = window.astype(BF16).astype(F32)
    middle = (window - high).astype(BF16).astype(F32)
    low = window - high - middle
    row = lax.broadcasted_iota(jnp.int32, (16, WIN), 0)
    split = jnp.where(row == 0, high, jnp.where(row == 1, middle, jnp.where(row == 2, low, 0.0))).astype(BF16)
    weight = jnp.sum(jnp.dot(split, picks, preferred_element_type=F32), 0, keepdims=True)
    rows = codes.shape[1]
    for part in range(2):
        moved = jnp.dot(codes[part, :, pl.ds(start, WIN)], picks, preferred_element_type=F32) * weight
        out[part] = moved.astype(BF16)
        if with_turned:
            turned[:, part * rows:part * rows + rows] = moved.T.astype(BF16)


def slots(by_row, with_turned, ranks, codes, scale):
    parts, rows, cap = codes.shape
    tiles = ranks.shape[0]
    out_specs = [pl.BlockSpec((parts, rows, BLK), lambda i: (0, 0, i))]
    out_shape = [jax.ShapeDtypeStruct((parts, rows, tiles * RSLOT), BF16)]
    if with_turned:
        out_specs.append(pl.BlockSpec((BLK, parts * rows), lambda i: (i, 0)))
        out_shape.append(jax.ShapeDtypeStruct((tiles * RSLOT, parts * rows), BF16))
    return pl.pallas_call(
        functools.partial(slot_kernel, by_row, with_turned),
        grid=(tiles * RSLOT // BLK,),
        in_specs=[
            pl.BlockSpec(memory_space=pltpu.SMEM),
            pl.BlockSpec((parts, rows, cap), lambda i: (0, 0, 0), pipeline_mode=pl.Buffered(1)),
            pl.BlockSpec((1, cap), lambda i: (0, 0)),
        ],
        out_specs=out_specs,
        out_shape=out_shape,
        scratch_shapes=[pltpu.SMEM((tiles,), jnp.int32), pltpu.SMEM((tiles,), jnp.int32)],
        compiler_params=pltpu.CompilerParams(vmem_limit_bytes=16 << 20),
        cost_estimate=pl.CostEstimate(flops=4 * cap * rows * WIN, bytes_accessed=2 * parts * rows * cap * 2, transcendentals=0),
        name="slot_rows" if by_row else "slot_cols",
    )(ranks, codes, scale)


def complex_rows(stacked, rows, lanes):
    half = lanes // 2
    imag = stacked[rows:]
    swapped = jnp.concatenate([imag[:, half:], imag[:, :half]], 1)
    sign = jnp.where(lax.broadcasted_iota(jnp.int32, (1, lanes), 1) < half, -1.0, 1.0)
    return stacked[:rows] + swapped * sign


def stream(source, target, sems, pieces):
    lead, rows, _ = source.shape
    step = rows // pieces
    todo = []
    for index in range(lead):
        for k in range(pieces):
            at = pl.ds(k * step, step)
            copy = pltpu.make_async_copy(source.at[index, at], target.at[index, at], sems.at[index * pieces + k])
            copy.start()
            todo.append((copy, index, k * step))
    return todo, step


def residual_kernel(coefs, factor, turned, data, out, held, held_turned, got, both, sems, more_sems):
    parts, rows, cap = factor.shape
    lanes = coefs.shape[1]
    half = lanes // 2
    todo, step = stream(factor, held, sems, sems.shape[0] // parts)
    later, later_step = stream(turned, held_turned, more_sems, more_sems.shape[0])
    for copy, part, at in todo:
        copy.wait()
        got[part * rows + at:part * rows + at + step] = jnp.dot(held[part, at:at + step], coefs[...], preferred_element_type=F32)
    predicted = complex_rows(got[...], rows, lanes)
    rest = (predicted - data[...].astype(F32)).astype(BF16).astype(F32)
    swapped = jnp.concatenate([rest[:, half:], rest[:, :half]], 1)
    sign = jnp.where(lax.broadcasted_iota(jnp.int32, (1, lanes), 1) < half, 1.0, -1.0)
    both[:rows] = rest.astype(BF16)
    both[rows:] = (swapped * sign).astype(BF16)
    for copy, _, at in later:
        copy.wait()
        out[at:at + later_step] = jnp.dot(held_turned[0, at:at + later_step], both[...], preferred_element_type=F32).astype(BF16)


def residual(coefs, factor, turned, data):
    parts, rows, cap = factor.shape
    lanes = coefs.shape[1]
    vmem, hbm = pl.BlockSpec(memory_space=pltpu.VMEM), pl.BlockSpec(memory_space=pl.ANY)
    factor, turned = in_hbm(factor, turned[None])
    return pl.pallas_call(
        residual_kernel,
        in_specs=[vmem, hbm, hbm, vmem],
        out_specs=vmem,
        out_shape=jax.ShapeDtypeStruct((cap, lanes), BF16),
        scratch_shapes=[
            pltpu.VMEM((parts, rows, cap), BF16),
            pltpu.VMEM((1, cap, parts * rows), BF16),
            pltpu.VMEM((parts * rows, lanes), F32),
            pltpu.VMEM((parts * rows, lanes), BF16),
            pltpu.SemaphoreType.DMA((2 * parts,)),
            pltpu.SemaphoreType.DMA((2,)),
        ],
        compiler_params=pltpu.CompilerParams(vmem_limit_bytes=32 << 20),
        cost_estimate=pl.CostEstimate(flops=8 * cap * rows * lanes, bytes_accessed=2 * cap * lanes * 2, transcendentals=0),
        name="residual",
    )(coefs, factor, turned, data)


def gradient_kernel(coefs, factor, out, held, got, sems):
    parts, rows, cap = factor.shape
    lanes = coefs.shape[1]
    todo, step = stream(factor, held, sems, sems.shape[0] // parts)
    for copy, part, at in todo:
        copy.wait()
        got[part * rows + at:part * rows + at + step] = jnp.dot(held[part, at:at + step], coefs[...], preferred_element_type=F32)
    flipped = complex_rows(got[...], rows, lanes).T
    owners, each, _ = out.shape
    half = each // 2
    for owner in range(owners):
        for ri in range(2):
            at = ri * (lanes // 2) + owner * half
            out[owner, ri * half:ri * half + half, :] = flipped[at:at + half].astype(BF16)


def gradient(coefs, factor, owners):
    parts, rows, cap = factor.shape
    lanes = coefs.shape[1]
    vmem = pl.BlockSpec(memory_space=pltpu.VMEM)
    return pl.pallas_call(
        gradient_kernel,
        in_specs=[vmem, pl.BlockSpec(memory_space=pl.ANY)],
        out_specs=vmem,
        out_shape=jax.ShapeDtypeStruct((owners, lanes // owners, rows), BF16),
        scratch_shapes=[
            pltpu.VMEM((parts, rows, cap), BF16),
            pltpu.VMEM((parts * rows, lanes), F32),
            pltpu.SemaphoreType.DMA((2 * parts,)),
        ],
        compiler_params=pltpu.CompilerParams(vmem_limit_bytes=20 << 20),
        cost_estimate=pl.CostEstimate(flops=4 * cap * rows * lanes, bytes_accessed=cap * lanes * 2, transcendentals=0),
        name="gradient",
    )(coefs, *in_hbm(factor))


def time_kernel(mute, arrived, basis, out, spectra):
    step = pl.program_id(0)
    here, share, times = out.shape
    depth = basis.shape[0]

    @pl.when(step == 0)
    def _():
        spectra[...] = arrived[...].reshape(depth, arrived.shape[2]).astype(F32).T

    lane = lax.broadcasted_iota(jnp.int32, (share, depth), 1)
    row = lax.broadcasted_iota(jnp.int32, (share, depth), 0)
    own = row == lane % share
    when = lax.broadcasted_iota(jnp.int32, (share, times), 1)
    base = step * here
    lines = []
    for n in range(here):
        lines.append(jnp.where(own, spectra[pl.ds(base + n, 1), :], 0.0).astype(BF16))
    got = jnp.dot(jnp.concatenate(lines, 0), basis[...], preferred_element_type=F32)
    signal = got[:, :times] + got[:, times:]
    for n in range(here):
        out[n] = jnp.where(when >= mute[base + n], signal[n * share:n * share + share], 0.0).astype(BF16)


def to_time(mute, arrived, basis, rows, share):
    block = 128
    return pl.pallas_call(
        time_kernel,
        grid=(rows // block,),
        in_specs=[
            pl.BlockSpec(memory_space=pltpu.SMEM),
            pl.BlockSpec(arrived.shape, lambda i: (0, 0, 0)),
            pl.BlockSpec(basis.shape, lambda i: (0, 0)),
        ],
        out_specs=pl.BlockSpec((block, share, NTIME), lambda i: (i, 0, 0)),
        out_shape=jax.ShapeDtypeStruct((rows, share, NTIME), BF16),
        scratch_shapes=[pltpu.VMEM((rows, basis.shape[0]), F32)],
        compiler_params=pltpu.CompilerParams(vmem_limit_bytes=16 << 20),
        name="to_time",
    )(mute, arrived, basis)


def shards(model_field, data_field, u_codes, u_scales, v_codes, v_scales, tile_ranks, mute_start):
    ranks = tile_ranks[0]
    tiles = ranks.shape[0]
    rows = model_field.shape[1]
    width = model_field.shape[2]
    freq_count = lax.axis_size("freq")
    sources = width // 2
    share = sources // freq_count
    basis = jnp.asarray(time_basis(freq_count, share))
    sent = coef(ranks, v_codes[0], v_scales[0], model_field[0])
    late_u, late_v, sent = lax.optimization_barrier((u_codes[0], v_codes[0], sent))
    arrived = lax.all_to_all(sent, "tile", split_axis=0, concat_axis=0, tiled=True)
    u_slots, u_turned = slots(True, True, ranks, late_u, u_scales[0])
    v_slots, = slots(False, False, ranks, late_v, v_scales[0])
    back = residual(arrived.reshape(tiles * RSLOT, width), u_slots, u_turned, data_field[0])
    back = lax.all_to_all(back.reshape(tiles, RSLOT, width), "tile", split_axis=0, concat_axis=0, tiled=True)
    part = gradient(back.reshape(tiles * RSLOT, width), v_slots, freq_count)
    spectra = lax.all_to_all(part, "freq", split_axis=0, concat_axis=0, tiled=True)
    return to_time(mute_start, spectra, basis, rows, share)


def solution(mesh):
    in_specs = (
        P("freq", "tile", None),
        P("freq", "tile", None),
        P("freq", None, "tile", None),
        P("freq", "tile", None),
        P("freq", None, "tile", None),
        P("freq", "tile", None),
        P("freq", None, None),
        P("tile"),
    )
    out_specs = P("tile", "freq", None)
    return jax.shard_map(shards, mesh=mesh, in_specs=in_specs, out_specs=out_specs, check_vma=False)
```

time: 173 us -> 126 us (0.73)
  other arithmetic: 59.4 us -> 0 us
  Pallas kernels: 0 us -> 38.8 us
  local copies, waits for them, and re-layouts: 43.4 us -> 12.8 us
  matrix products: 18.6 us -> 0 us
  waiting for transfers between devices: 21.9 us -> 40.4 us
  blocking collectives: 0 us -> 14.1 us
  starting transfers between devices: 28 us -> 19.8 us
    gather x10 -> x0, other arithmetic: 41.7 us -> none  [the longest x6 41.7 us: pool_owner(): offset = column - begins[owner_tile]]
    pallas_call x0 -> x6, Pallas kernels: none -> 38.8 us  [the longest x2 15.1 us: slots(): pl.pallas_call(functools.partial(slot_kernel, by_row, with_turned), grid=...]
    gather x8 -> x0, local copies, waits for them, and re-layouts: 36 us -> none  [the longest x2 16.5 us: fill_slots(): pooled[source.reshape(-1)]]
    dot_general x9 -> x0, matrix products: 18.6 us -> none  [the longest x2 6.33 us: apply_factor(): real_part = jnp.dot(factor[0], pooled, preferred_element_type=jnp.float32)]
    all_to_all x3 -> x2, waiting for transfers between devices: 21.9 us -> 40.4 us  [the longest x1 22 us: shards(): lax.all_to_all(back.reshape(tiles, RSLOT, width), 'tile', split_axis=0, c...]
    all_to_all x0 -> x1, blocking collectives: none -> 14.1 us  [shards(): lax.all_to_all(part, 'freq', split_axis=0, concat_axis=0, tiled=True)]
    unnamed x15 -> x22, local copies, waits for them, and re-layouts: 1.9 us -> 12.8 us
    convert_element_type x3 -> x0, other arithmetic: 9.93 us -> none  [the longest x2 9.92 us: unpack_pool(): return (code_vals.astype(jnp.float32) * scale_row).astype(jnp.bfloat16)]
  transfers between devices with their start and end apart: 3 -> 2, of which waited for: 3 -> 2; matrix products, arithmetic and copies ran while one was open for 30% -> 0% of each run, Pallas kernels for 0% -> 12%
where the time goes in v1:
time: 126 us
  waiting for transfers between devices  40.4 us (32%)
  Pallas kernels  38.8 us (31%)
  starting transfers between devices  19.8 us (16%)
  blocking collectives  14.1 us (11%)
  local copies, waits for them, and re-layouts  12.8 us (10%)
    all_to_all x1, waiting for transfers between devices, shards(): lax.all_to_all(back.reshape(tiles, RSLOT, width), 'tile', split_axis=0, c...  22 us
    all_to_all x1, waiting for transfers between devices, shards(): lax.all_to_all(sent, 'tile', split_axis=0, concat_axis=0, tiled=True)  18.3 us
    pallas_call x2, Pallas kernels, slots(): pl.pallas_call(functools.partial(slot_kernel, by_row, with_turned), grid=...  15.1 us
    all_to_all x1, blocking collectives, shards(): lax.all_to_all(part, 'freq', split_axis=0, concat_axis=0, tiled=True)  14.1 us
    unnamed x22, local copies, waits for them, and re-layouts  12.8 us
    all_to_all x1, starting transfers between devices, shards(): lax.all_to_all(sent, 'tile', split_axis=0, concat_axis=0, tiled=True)  12.2 us
    pallas_call x1, Pallas kernels, residual(): pl.pallas_call(residual_kernel, in_specs=[vmem, hbm, hbm, vmem], out_spec...  9.41 us
    all_to_all x1, starting transfers between devices, shards(): lax.all_to_all(back.reshape(tiles, RSLOT, width), 'tile', split_axis=0, c...  7.58 us
  transfers between devices with their start and end apart: 2, of which 2 were waited for; matrix products, arithmetic and copies ran while one was open for 0% of the time, Pallas kernels for 12%

profile of v1, /device:TPU:1, one launch (start us, length us, event | category | flops | bytes accessed | tf_op | source)
XLA Modules:
  0.0 125.9 jit_solution(11215185696393096496)
XLA Ops:
  0.0 5.5 %coef.1 = bf16[32,88,256]{2,1,0:T(8,128)(2,1)} custom-call(s32[32,32]{1,0:T(8,128)} %bitcast.17, bf16[2,512,2816]{2,1,0:T(8,128)(2,1)} %bitcast.11, f32[1,2816]{1,0:T(1,128)} %bitcast.20, bf16[512,256]{1,0:T(8,128)(2,1)} %bitcast.24), custom_call_target="tpu_custom_call" | custom-call | flops 1476395008 | bytes 5767168 | tf_op jit(solution)/shard_map/coef/pallas_call | solution.py:83
  5.6 0.0 copy-start.4
  5.6 12.2 %all-to-all-start = ((bf16[32,88,256]{2,1,0:T(8,128)(2,1)}), bf16[32,88,256]{2,1,0:T(8,128)(2,1)S(1)}, u32[]{:S(2)}, u32[]{:S(2)}) async-start(bf16[32,88,256]{2,1,0:T(8,128)(2,1)} %coef.1), calls=%async_computation | async-start | bytes 2883584 | tf_op jit(solution)/shard_map/all_to_all | solution.py:329
  17.8 0.0 copy-done.6
  17.8 0.0 copy-done.10
  17.8 0.0 copy-start.9
  17.8 2.6 %copy-done.9 = bf16[1,2,512,2816]{3,2,1,0:T(8,128)(2,1)S(1)} copy-done((bf16[1,2,512,2816]{3,2,1,0:T(8,128)(2,1)S(1)}, bf16[1,2,512,2816]{3,2,1,0:T(8,128)(2,1)}, u32[]{:S(2)}) %copy-start.9) | copy-done | bytes 5767192
  20.4 8.0 %slot_rows.1 = (bf16[2,512,2816]{2,1,0:T(8,128)(2,1)S(1)}, bf16[2816,1024]{1,0:T(8,128)(2,1)S(1)}) custom-call(s32[32,32]{1,0:T(8,128)S(1)} %bitcast.18, bf16[2,512,2816]{2,1,0:T(8,128)(2,1)S(1)} %bitcast.22, f32[1,2816]{1,0:T(1,128)S(1)} %bitcast.23), custom_call_target="tpu_custom_call" | custom-call | flops 2214592512 | bytes 11534336 | tf_op jit(solution)/shard_map/slot_rows/pallas_call | solution.py:159
  28.5 0.0 copy-start.2
  28.5 2.5 %copy-done.2 = bf16[2,512,2816]{2,1,0:T(8,128)(2,1)} copy-done((bf16[2,512,2816]{2,1,0:T(8,128)(2,1)}, bf16[2,512,2816]{2,1,0:T(8,128)(2,1)S(1)}, u32[]{:S(2)}) %copy-start.2) | copy-done | bytes 5767192
  31.0 2.5 %copy-done.3 = bf16[2816,1024]{1,0:T(8,128)(2,1)} copy-done((bf16[2816,1024]{1,0:T(8,128)(2,1)}, bf16[2816,1024]{1,0:T(8,128)(2,1)S(1)}, u32[]{:S(2)}) %copy-start.3) | copy-done | bytes 5767192
  33.5 18.3 %all-to-all-done = bf16[32,88,256]{2,1,0:T(8,128)(2,1)S(1)} async-done(((bf16[32,88,256]{2,1,0:T(8,128)(2,1)}), bf16[32,88,256]{2,1,0:T(8,128)(2,1)S(1)}, u32[]{:S(2)}, u32[]{:S(2)}) %all-to-all-start) | async-done | bytes 1441824 | tf_op jit(solution)/shard_map/all_to_all | solution.py:329
  51.8 0.0 copy-done.4
  51.8 9.4 %residual.1 = bf16[2816,256]{1,0:T(8,128)(2,1)} custom-call(bf16[2816,256]{1,0:T(8,128)(2,1)S(1)} %bitcast.13, bf16[2,512,2816]{2,1,0:T(8,128)(2,1)} %copy-done.2, bf16[1,2816,1024]{2,1,0:T(8,128)(2,1)} %bitcast.14, bf16[512,256]{1,0:T(8,128)(2,1)S(1)} %bitcast.16), custom_call_target="tpu_custom_call" | custom-call | flops 2952790016 | bytes 2883584 | tf_op jit(solution)/shard_map/residual/pallas_call | solution.py:222
  61.2 7.6 %all-to-all-start.1 = ((bf16[32,88,256]{2,1,0:T(8,128)(2,1)}), bf16[32,88,256]{2,1,0:T(8,128)(2,1)S(1)}, u32[]{:S(2)}, u32[]{:S(2)}) async-start(bf16[32,88,256]{2,1,0:T(8,128)(2,1)} %bitcast.9), calls=%async_computation.1 | async-start | bytes 2883584 | tf_op jit(solution)/shard_map/all_to_all | solution.py:333
  68.8 0.0 copy-done.7
  68.8 0.0 copy-start
  68.8 2.6 %copy-done = bf16[1,2,512,2816]{3,2,1,0:T(8,128)(2,1)S(1)} copy-done((bf16[1,2,512,2816]{3,2,1,0:T(8,128)(2,1)S(1)}, bf16[1,2,512,2816]{3,2,1,0:T(8,128)(2,1)}, u32[]{:S(2)}) %copy-start) | copy-done | bytes 5767192
  71.5 7.0 %slot_cols.1.factor = bf16[2,512,2816]{2,1,0:T(8,128)(2,1)S(1)} custom-call(s32[32,32]{1,0:T(8,128)S(1)} %bitcast.19, bf16[2,512,2816]{2,1,0:T(8,128)(2,1)S(1)} %bitcast.12, f32[1,2816]{1,0:T(1,128)S(1)} %bitcast.21), custom_call_target="tpu_custom_call" | custom-call | flops 2214592512 | bytes 11534336 | tf_op jit(solution)/shard_map/slot_cols/pallas_call | solution.py:159
  78.5 2.5 %copy-done.1 = bf16[2,512,2816]{2,1,0:T(8,128)(2,1)} copy-done((bf16[2,512,2816]{2,1,0:T(8,128)(2,1)}, bf16[2,512,2816]{2,1,0:T(8,128)(2,1)S(1)}, u32[]{:S(2)}) %copy-start.1) | copy-done | bytes 5767192
  81.0 22.0 %all-to-all-done.1 = bf16[32,88,256]{2,1,0:T(8,128)(2,1)S(1)} async-done(((bf16[32,88,256]{2,1,0:T(8,128)(2,1)}), bf16[32,88,256]{2,1,0:T(8,128)(2,1)S(1)}, u32[]{:S(2)}, u32[]{:S(2)}) %all-to-all-start.1) | async-done | bytes 1441824 | tf_op jit(solution)/shard_map/all_to_all | solution.py:333
  103.0 5.0 %gradient.1 = bf16[8,32,512]{2,1,0:T(8,128)(2,1)S(1)} custom-call(bf16[2816,256]{1,0:T(8,128)(2,1)S(1)} %bitcast.15, bf16[2,512,2816]{2,1,0:T(8,128)(2,1)} %copy-done.1), custom_call_target="tpu_custom_call" | custom-call | flops 1476395008 | bytes 1441792 | tf_op jit(solution)/shard_map/gradient/pallas_call | solution.py:261
  108.1 14.1 %all_to_all.15.arrived = bf16[8,32,512]{2,1,0:T(8,128)(2,1)S(1)} all-to-all(bf16[8,32,512]{2,1,0:T(8,128)(2,1)S(1)} %gradient.1), channel_id=1, replica_groups=mesh['freq'=8,'tile'=32] {'freq'}, dimensions={0} | all-to-all | bytes 524288 | tf_op jit(solution)/shard_map/all_to_all | solution.py:335
  122.2 3.7 %to_time.1 = bf16[512,16,128]{2,1,0:T(8,128)(2,1)} custom-call(s32[512]{0:T(512)S(1)} %copy-done.8, bf16[8,32,512]{2,1,0:T(8,128)(2,1)S(1)} %all_to_all.15.arrived, bf16[256,256]{1,0:T(8,128)(2,1)S(1)} %copy-done.5), custom_call_target="tpu_custom_call" | custom-call | tf_op jit(solution)/shard_map/to_time/pallas_call | solution.py:302
  (9 shorter events, 0.0 us)
Async XLA Ops:
  0.0 17.8 %copy-start.6 = (s32[1,32,32]{2,1,0:T(8,128)S(1)}, s32[1,32,32]{2,1,0:T(8,128)}, u32[]{:S(2)}) copy-start(s32[1,32,32]{2,1,0:T(8,128)} %param.15) | copy-start | bytes 12292
  0.0 17.8 %copy-start.10 = (f32[1,1,2816]{2,1,0:T(1,128)S(1)}, f32[1,1,2816]{2,1,0:T(1,128)}, u32[]{:S(2)}) copy-start(f32[1,1,2816]{2,1,0:T(1,128)} %param.12) | copy-start | bytes 33796
  5.6 46.3 %copy-start.4 = (bf16[1,512,256]{2,1,0:T(8,128)(2,1)S(1)}, bf16[1,512,256]{2,1,0:T(8,128)(2,1)}, u32[]{:S(2)}) copy-start(bf16[1,512,256]{2,1,0:T(8,128)(2,1)} %param.10) | copy-start | bytes 786436
  5.6 46.2 %all-to-all-start = ((bf16[32,88,256]{2,1,0:T(8,128)(2,1)}), bf16[32,88,256]{2,1,0:T(8,128)(2,1)S(1)}, u32[]{:S(2)}, u32[]{:S(2)}) async-start(bf16[32,88,256]{2,1,0:T(8,128)(2,1)} %coef.1), calls=%async_computation | async-start | bytes 2883584 | tf_op jit(solution)/shard_map/all_to_all | solution.py:329
  17.8 2.6 %copy-start.9 = (bf16[1,2,512,2816]{3,2,1,0:T(8,128)(2,1)S(1)}, bf16[1,2,512,2816]{3,2,1,0:T(8,128)(2,1)}, u32[]{:S(2)}) copy-start(bf16[1,2,512,2816]{3,2,1,0:T(8,128)(2,1)} %param.11) | copy-start | bytes 17301508
  28.5 2.5 %copy-start.2 = (bf16[2,512,2816]{2,1,0:T(8,128)(2,1)}, bf16[2,512,2816]{2,1,0:T(8,128)(2,1)S(1)}, u32[]{:S(2)}) copy-start(bf16[2,512,2816]{2,1,0:T(8,128)(2,1)S(1)} %get-tuple-element.12.factor) | copy-start | bytes 17301508
  31.0 2.5 %copy-start.3 = (bf16[2816,1024]{1,0:T(8,128)(2,1)}, bf16[2816,1024]{1,0:T(8,128)(2,1)S(1)}, u32[]{:S(2)}) copy-start(bf16[2816,1024]{1,0:T(8,128)(2,1)S(1)} %get-tuple-element.13) | copy-start | bytes 17301508
  51.8 17.0 %copy-start.7 = (f32[1,1,2816]{2,1,0:T(1,128)S(1)}, f32[1,1,2816]{2,1,0:T(1,128)}, u32[]{:S(2)}) copy-start(f32[1,1,2816]{2,1,0:T(1,128)} %param.14) | copy-start | bytes 33796
  61.2 41.8 %all-to-all-start.1 = ((bf16[32,88,256]{2,1,0:T(8,128)(2,1)}), bf16[32,88,256]{2,1,0:T(8,128)(2,1)S(1)}, u32[]{:S(2)}, u32[]{:S(2)}) async-start(bf16[32,88,256]{2,1,0:T(8,128)(2,1)} %bitcast.9), calls=%async_computation.1 | async-start | bytes 2883584 | tf_op jit(solution)/shard_map/all_to_all | solution.py:333
  68.8 2.6 %copy-start = (bf16[1,2,512,2816]{3,2,1,0:T(8,128)(2,1)S(1)}, bf16[1,2,512,2816]{3,2,1,0:T(8,128)(2,1)}, u32[]{:S(2)}) copy-start(bf16[1,2,512,2816]{3,2,1,0:T(8,128)(2,1)} %param.13) | copy-start | bytes 17301508
  78.5 2.5 %copy-start.1 = (bf16[2,512,2816]{2,1,0:T(8,128)(2,1)}, bf16[2,512,2816]{2,1,0:T(8,128)(2,1)S(1)}, u32[]{:S(2)}) copy-start(bf16[2,512,2816]{2,1,0:T(8,128)(2,1)S(1)} %slot_cols.1.factor) | copy-start | bytes 17301508
  81.0 41.2 %copy-start.5 = (bf16[256,256]{1,0:T(8,128)(2,1)S(1)}, bf16[256,256]{1,0:T(8,128)(2,1)}, u32[]{:S(2)}) copy-start(bf16[256,256]{1,0:T(8,128)(2,1)} %constant.2.clone.basis) | copy-start | bytes 393220
  81.0 41.2 %copy-start.8 = (s32[512]{0:T(512)S(1)}, s32[512]{0:T(512)}, u32[]{:S(2)}) copy-start(s32[512]{0:T(512)} %mute.1) | copy-start | bytes 6148

commit v2 on v1

v2 whole, which is shorter than its diff:
```python
import functools
import math

import jax
import jax.numpy as jnp
import numpy as np
from jax import lax
from jax.experimental import pallas as pl
from jax.experimental.pallas import tpu as pltpu
from jax.sharding import PartitionSpec as P

RSLOT = 88
NTIME = 128
BLK = 256
WIN = 384
TIME_PIECES = 4
OUT_PIECES = 4
TURNED_PIECES = 2
F32 = jnp.float32
BF16 = jnp.bfloat16
NT_DIMS = (((1,), (1,)), ((), ()))


def time_basis(freq_count, per):
    arg = 2.0 * math.pi * (np.arange(freq_count)[:, None] + 1.0) * np.arange(NTIME)[None, :] / NTIME
    base = 0.5 * np.stack([np.cos(arg), -np.sin(arg)], 1)
    rows = np.repeat(base.reshape(freq_count * 2, NTIME), per, 0).astype(np.float32)
    high = rows.astype(jnp.bfloat16)
    low = (rows - high.astype(np.float32)).astype(jnp.bfloat16)
    return np.concatenate([high, low], 1)


def start_all(*copies):
    for copy in copies:
        copy.start()
    return copies


def coef_kernel(ranks, codes, scale, model, out, plain, rotated, first, pool, ready, out_sems):
    part = pl.program_id(0)
    _, rows, cap = codes.shape
    tiles = ranks.shape[0]
    half = model.shape[1] // 2
    mine = lax.axis_index("tile")
    piece = cap // 2

    @pl.when(part == 0)
    def _():
        for lane in range(2):
            pool[lane, cap:cap + RSLOT + 8, :] = jnp.zeros((RSLOT + 8, 128), F32)
        turned = model[...].astype(F32).T
        plain[...] = turned.astype(BF16)
        rotated[:half] = turned[half:].astype(BF16)
        rotated[half:] = (-turned[:half]).astype(BF16)
        for at in range(0, cap, piece):
            first[:, at:at + piece] = jnp.dot(plain[...], codes[0, :, at:at + piece], preferred_element_type=F32)

    def move(tile, begin):
        for lane in range(2):
            ready[tile, :, lane * 128:lane * 128 + 128] = pool[lane, pl.ds(begin, RSLOT), :].astype(BF16)
        return begin + ranks[tile, mine]

    @pl.when(part == 1)
    def _():
        for at in range(0, cap, piece):
            acc = first[:, at:at + piece] + jnp.dot(rotated[...], codes[0, :, at:at + piece], preferred_element_type=F32)
            upright = (acc * scale[:, at:at + piece]).T
            for lane in range(2):
                pool[lane, at:at + piece, :] = upright[:, lane * 128:lane * 128 + 128]
        begin = jnp.int32(0)
        leaving = []
        per = tiles // OUT_PIECES
        for k in range(OUT_PIECES):
            begin = lax.fori_loop(k * per, k * per + per, move, begin)
            leaving.append(pltpu.make_async_copy(ready.at[pl.ds(k * per, per)], out.at[pl.ds(k * per, per)], out_sems.at[k]))
            leaving[-1].start()
        for copy in leaving:
            copy.wait()


def in_hbm(*arrays):
    return [pltpu.with_memory_space_constraint(array, pltpu.HBM) for array in arrays]


def coef(ranks, codes, scale, model):
    parts, rows, cap = codes.shape
    width = model.shape[1]
    tiles = ranks.shape[0]
    return pl.pallas_call(
        coef_kernel,
        grid=(parts,),
        in_specs=[
            pl.BlockSpec(memory_space=pltpu.SMEM),
            pl.BlockSpec((1, rows, cap), lambda i: (i, 0, 0)),
            pl.BlockSpec(scale.shape, lambda i: (0, 0)),
            pl.BlockSpec(model.shape, lambda i: (0, 0)),
        ],
        out_specs=pl.BlockSpec(memory_space=pl.ANY),
        out_shape=jax.ShapeDtypeStruct((tiles, RSLOT, width), BF16),
        scratch_shapes=[
            pltpu.VMEM((width, rows), BF16),
            pltpu.VMEM((width, rows), BF16),
            pltpu.VMEM((width, cap), F32),
            pltpu.VMEM((2, cap + RSLOT + 8, 128), F32),
            pltpu.VMEM((tiles, RSLOT, width), BF16),
            pltpu.SemaphoreType.DMA((OUT_PIECES,)),
        ],
        compiler_params=pltpu.CompilerParams(vmem_limit_bytes=32 << 20),
        cost_estimate=pl.CostEstimate(flops=4 * cap * rows * width, bytes_accessed=parts * rows * cap * 2, transcendentals=0),
        name="coef",
    )(*in_hbm(ranks, codes, scale, model))


def slot_kernel(by_row, with_turned, ranks, codes, scale, *rest):
    out = rest[0]
    turned = rest[1] if with_turned else None
    begin, rank = rest[-2:]
    step = pl.program_id(0)
    tiles = ranks.shape[0]
    cap = codes.shape[2]
    mine = lax.axis_index("tile")

    @pl.when(step == 0)
    def _():
        def fill(tile, acc):
            here = ranks[mine, tile] if by_row else ranks[tile, mine]
            begin[tile] = acc
            rank[tile] = here
            return acc + here

        lax.fori_loop(0, tiles, fill, jnp.int32(0))

    first_tile = (step * BLK) // RSLOT
    inside = step * BLK - first_tile * RSLOT
    first = begin[first_tile] + jnp.minimum(inside, rank[first_tile])
    start = pl.multiple_of(jnp.minimum((first // 128) * 128, cap - WIN), 128)
    lane = lax.broadcasted_iota(jnp.int32, (1, BLK), 1)
    where_from = jnp.full((1, BLK), -1, jnp.int32)
    for ahead in range(-(-BLK // RSLOT) + 1):
        tile = jnp.minimum(first_tile + ahead, tiles - 1)
        offset = lane + (step * BLK - tile * RSLOT)
        live = (offset >= 0) & (offset < rank[tile])
        where_from = jnp.where(live, offset + (begin[tile] - start), where_from)
    picks = jnp.where(lax.broadcasted_iota(jnp.int32, (WIN, BLK), 0) == where_from, 1.0, 0.0).astype(BF16)
    window = scale[:, pl.ds(start, WIN)]
    high = window.astype(BF16).astype(F32)
    middle = (window - high).astype(BF16).astype(F32)
    low = window - high - middle
    row = lax.broadcasted_iota(jnp.int32, (16, WIN), 0)
    split = jnp.where(row == 0, high, jnp.where(row == 1, middle, jnp.where(row == 2, low, 0.0))).astype(BF16)
    weight = jnp.sum(jnp.dot(split, picks, preferred_element_type=F32), 0, keepdims=True)
    rows = codes.shape[1]
    for part in range(2):
        moved = jnp.dot(codes[part, :, pl.ds(start, WIN)], picks, preferred_element_type=F32) * weight
        out[part] = moved.astype(BF16)
        if with_turned:
            turned[:, part * rows:part * rows + rows] = moved.T.astype(BF16)


def slots(by_row, with_turned, ranks, codes, scale):
    parts, rows, cap = codes.shape
    tiles = ranks.shape[0]
    out_specs = [pl.BlockSpec((parts, rows, BLK), lambda i: (0, 0, i))]
    out_shape = [jax.ShapeDtypeStruct((parts, rows, tiles * RSLOT), BF16)]
    if with_turned:
        out_specs.append(pl.BlockSpec((BLK, parts * rows), lambda i: (i, 0)))
        out_shape.append(jax.ShapeDtypeStruct((tiles * RSLOT, parts * rows), BF16))
    return pl.pallas_call(
        functools.partial(slot_kernel, by_row, with_turned),
        grid=(tiles * RSLOT // BLK,),
        in_specs=[
            pl.BlockSpec(memory_space=pltpu.SMEM),
            pl.BlockSpec((parts, rows, cap), lambda i: (0, 0, 0), pipeline_mode=pl.Buffered(1)),
            pl.BlockSpec((1, cap), lambda i: (0, 0)),
        ],
        out_specs=out_specs,
        out_shape=out_shape,
        scratch_shapes=[pltpu.SMEM((tiles,), jnp.int32), pltpu.SMEM((tiles,), jnp.int32)],
        compiler_params=pltpu.CompilerParams(vmem_limit_bytes=16 << 20),
        cost_estimate=pl.CostEstimate(flops=4 * cap * rows * WIN, bytes_accessed=2 * parts * rows * cap * 2, transcendentals=0),
        name="slot_rows" if by_row else "slot_cols",
    )(ranks, codes, scale)


def complex_rows(stacked, rows, lanes):
    half = lanes // 2
    imag = stacked[rows:]
    swapped = jnp.concatenate([imag[:, half:], imag[:, :half]], 1)
    sign = jnp.where(lax.broadcasted_iota(jnp.int32, (1, lanes), 1) < half, -1.0, 1.0)
    return stacked[:rows] + swapped * sign


def residual_kernel(coefs, factor, turned, data, out, held, real, both, ready, sems, out_sems):
    part = pl.program_id(0)
    _, rows, cap = factor.shape
    lanes = coefs.shape[1]
    half = lanes // 2
    step = cap // TURNED_PIECES
    copies = []
    for k in range(TURNED_PIECES):
        at = pl.ds(k * step, step)
        copies.append(pltpu.make_async_copy(turned.at[at], held.at[at], sems.at[k]))

    @pl.when(part == 0)
    def _():
        for copy in copies:
            copy.start()
        real[...] = jnp.dot(factor[0], coefs[...], preferred_element_type=F32)

    @pl.when(part == 1)
    def _():
        imag = jnp.dot(factor[0], coefs[...], preferred_element_type=F32)
        side = lax.broadcasted_iota(jnp.int32, (1, lanes), 1) < half
        swapped = jnp.concatenate([imag[:, half:], imag[:, :half]], 1)
        rest = (real[...] + swapped * jnp.where(side, -1.0, 1.0) - data[...].astype(F32)).astype(BF16).astype(F32)
        swapped = jnp.concatenate([rest[:, half:], rest[:, :half]], 1)
        both[:rows] = rest.astype(BF16)
        both[rows:] = (swapped * jnp.where(side, 1.0, -1.0)).astype(BF16)
        leaving = []
        weights = both[...]
        for k in range(TURNED_PIECES):
            copies[k].wait()
            at = slice(k * step, k * step + step)
            ready[at] = jnp.dot(held[at], weights, preferred_element_type=F32).astype(BF16)
            leaving.append(pltpu.make_async_copy(ready.at[at], out.at[at], out_sems.at[k]))
            leaving[-1].start()
        for copy in leaving:
            copy.wait()


def residual(coefs, factor, turned, data):
    parts, rows, cap = factor.shape
    lanes = coefs.shape[1]
    hbm = pl.BlockSpec(memory_space=pl.ANY)
    return pl.pallas_call(
        residual_kernel,
        grid=(parts,),
        in_specs=[
            pl.BlockSpec((cap, lanes), lambda i: (0, 0)),
            pl.BlockSpec((1, rows, cap), lambda i: (i, 0, 0)),
            hbm,
            pl.BlockSpec((rows, lanes), lambda i: (0, 0)),
        ],
        out_specs=hbm,
        out_shape=jax.ShapeDtypeStruct((cap, lanes), BF16),
        scratch_shapes=[
            pltpu.VMEM((cap, parts * rows), BF16),
            pltpu.VMEM((rows, lanes), F32),
            pltpu.VMEM((parts * rows, lanes), BF16),
            pltpu.VMEM((cap, lanes), BF16),
            pltpu.SemaphoreType.DMA((TURNED_PIECES,)),
            pltpu.SemaphoreType.DMA((TURNED_PIECES,)),
        ],
        compiler_params=pltpu.CompilerParams(vmem_limit_bytes=32 << 20),
        cost_estimate=pl.CostEstimate(flops=8 * cap * rows * lanes, bytes_accessed=2 * cap * lanes * 2, transcendentals=0),
        name="residual",
    )(coefs, *in_hbm(factor, turned), data)


def gradient_kernel(coefs, factor, out, real):
    part = pl.program_id(0)
    _, rows, cap = factor.shape
    lanes = coefs.shape[1]

    @pl.when(part == 0)
    def _():
        real[...] = jnp.dot(factor[0], coefs[...], preferred_element_type=F32)

    @pl.when(part == 1)
    def _():
        imag = jnp.dot(factor[0], coefs[...], preferred_element_type=F32)
        half_lanes = lanes // 2
        swapped = jnp.concatenate([imag[:, half_lanes:], imag[:, :half_lanes]], 1)
        sign = jnp.where(lax.broadcasted_iota(jnp.int32, (1, lanes), 1) < half_lanes, -1.0, 1.0)
        flipped = (real[...] + swapped * sign).T
        owners, each, _ = out.shape
        half = each // 2
        for owner in range(owners):
            for ri in range(2):
                at = ri * (lanes // 2) + owner * half
                out[owner, ri * half:ri * half + half, :] = flipped[at:at + half].astype(BF16)


def gradient(coefs, factor, owners):
    parts, rows, cap = factor.shape
    lanes = coefs.shape[1]
    return pl.pallas_call(
        gradient_kernel,
        grid=(parts,),
        in_specs=[pl.BlockSpec((cap, lanes), lambda i: (0, 0)), pl.BlockSpec((1, rows, cap), lambda i: (i, 0, 0))],
        out_specs=pl.BlockSpec((owners, lanes // owners, rows), lambda i: (0, 0, 0)),
        out_shape=jax.ShapeDtypeStruct((owners, lanes // owners, rows), BF16),
        scratch_shapes=[pltpu.VMEM((rows, lanes), F32)],
        compiler_params=pltpu.CompilerParams(vmem_limit_bytes=20 << 20),
        cost_estimate=pl.CostEstimate(flops=4 * cap * rows * lanes, bytes_accessed=cap * lanes * 2, transcendentals=0),
        name="gradient",
    )(coefs, *in_hbm(factor))


def time_kernel(mute, arrived, basis, out, spectra, ready, sems):
    rows, share, times = ready.shape
    depth = basis.shape[0]
    here = rows // sems.shape[0]
    spectra[...] = arrived[...].reshape(depth, rows).astype(F32).T
    lane = lax.broadcasted_iota(jnp.int32, (share, depth), 1)
    row = lax.broadcasted_iota(jnp.int32, (share, depth), 0)
    own = row == lane % share
    when = lax.broadcasted_iota(jnp.int32, (share, times), 1)

    def leaving(step):
        at = pl.ds(step * here, here)
        return pltpu.make_async_copy(ready.at[at], out.at[at], sems.at[step])

    def push(step, carry):
        base = step * here
        lines = []
        for n in range(here):
            lines.append(jnp.where(own, spectra[pl.ds(base + n, 1), :], 0.0).astype(BF16))
        got = jnp.dot(jnp.concatenate(lines, 0), basis[...], preferred_element_type=F32)
        signal = got[:, :times] + got[:, times:]
        for n in range(here):
            ready[base + n] = jnp.where(when >= mute[base + n], signal[n * share:n * share + share], 0.0).astype(BF16)
        leaving(step).start()
        return carry

    def finish(step, carry):
        leaving(step).wait()
        return carry

    lax.fori_loop(0, sems.shape[0], push, 0)
    lax.fori_loop(0, sems.shape[0], finish, 0)


def to_time(mute, arrived, basis, rows, share):
    vmem = pl.BlockSpec(memory_space=pltpu.VMEM)
    return pl.pallas_call(
        time_kernel,
        in_specs=[pl.BlockSpec(memory_space=pltpu.SMEM), vmem, vmem],
        out_specs=pl.BlockSpec(memory_space=pl.ANY),
        out_shape=jax.ShapeDtypeStruct((rows, share, NTIME), BF16),
        scratch_shapes=[
            pltpu.VMEM((rows, basis.shape[0]), F32),
            pltpu.VMEM((rows, share, NTIME), BF16),
            pltpu.SemaphoreType.DMA((TIME_PIECES,)),
        ],
        compiler_params=pltpu.CompilerParams(vmem_limit_bytes=16 << 20),
        name="to_time",
    )(mute, arrived, basis)


def shards(model_field, data_field, u_codes, u_scales, v_codes, v_scales, tile_ranks, mute_start):
    ranks = tile_ranks[0]
    tiles = ranks.shape[0]
    rows = model_field.shape[1]
    width = model_field.shape[2]
    freq_count = lax.axis_size("freq")
    sources = width // 2
    share = sources // freq_count
    basis = jnp.asarray(time_basis(freq_count, share))
    sent = coef(ranks, v_codes[0], v_scales[0], model_field[0])
    late_u, late_v, sent = lax.optimization_barrier((u_codes[0], v_codes[0], sent))
    arrived = lax.all_to_all(sent, "tile", split_axis=0, concat_axis=0, tiled=True)
    u_slots, u_turned = slots(True, True, ranks, late_u, u_scales[0])
    v_slots, = slots(False, False, ranks, late_v, v_scales[0])
    back = residual(arrived.reshape(tiles * RSLOT, width), u_slots, u_turned, data_field[0])
    back = lax.all_to_all(back.reshape(tiles, RSLOT, width), "tile", split_axis=0, concat_axis=0, tiled=True)
    part = gradient(back.reshape(tiles * RSLOT, width), v_slots, freq_count)
    spectra = lax.all_to_all(part, "freq", split_axis=0, concat_axis=0, tiled=True)
    return to_time(mute_start, spectra, basis, rows, share)


def solution(mesh):
    in_specs = (
        P("freq", "tile", None),
        P("freq", "tile", None),
        P("freq", None, "tile", None),
        P("freq", "tile", None),
        P("freq", None, "tile", None),
        P("freq", "tile", None),
        P("freq", None, None),
        P("tile"),
    )
    out_specs = P("tile", "freq", None)
    return jax.shard_map(shards, mesh=mesh, in_specs=in_specs, out_specs=out_specs, check_vma=False)
```

time: 126 us -> 123 us (0.976)
  Pallas kernels: 38.8 us -> 35.3 us
    pallas_call x4, Pallas kernels: 23.7 us -> 20.2 us  [the longest x1 7.86 us: residual(): pl.pallas_call(residual_kernel, grid=(parts,), in_specs=[pl.BlockSpec((ca...]
where the time goes in v2:
time: 123 us; the launch traced here: 122 us
  waiting for transfers between devices  40.4 us (33%)
  Pallas kernels  35.3 us (29%)
  starting transfers between devices  19.8 us (16%)
  blocking collectives  14.1 us (11%)
  local copies, waits for them, and re-layouts  12.8 us (10%)
    all_to_all x1, waiting for transfers between devices, shards(): lax.all_to_all(back.reshape(tiles, RSLOT, width), 'tile', split_axis=0, c...  22 us
    all_to_all x1, waiting for transfers between devices, shards(): lax.all_to_all(sent, 'tile', split_axis=0, concat_axis=0, tiled=True)  18.3 us
    pallas_call x2, Pallas kernels, slots(): pl.pallas_call(functools.partial(slot_kernel, by_row, with_turned), grid=...  15.1 us
    all_to_all x1, blocking collectives, shards(): lax.all_to_all(part, 'freq', split_axis=0, concat_axis=0, tiled=True)  14.1 us
    unnamed x22, local copies, waits for them, and re-layouts  12.8 us
    all_to_all x1, starting transfers between devices, shards(): lax.all_to_all(sent, 'tile', split_axis=0, concat_axis=0, tiled=True)  12.2 us
    pallas_call x1, Pallas kernels, residual(): pl.pallas_call(residual_kernel, grid=(parts,), in_specs=[pl.BlockSpec((ca...  7.86 us
    all_to_all x1, starting transfers between devices, shards(): lax.all_to_all(back.reshape(tiles, RSLOT, width), 'tile', split_axis=0, c...  7.58 us
  transfers between devices with their start and end apart: 2, of which 2 were waited for; matrix products, arithmetic and copies ran while one was open for 0% of the time, Pallas kernels for 12%

profile of v2, /device:TPU:1, one launch (start us, length us, event | category | flops | bytes accessed | tf_op | source)
XLA Modules:
  0.0 122.4 jit_solution(11926927494093141407)
XLA Ops:
  0.0 5.3 %coef.1 = bf16[32,88,256]{2,1,0:T(8,128)(2,1)} custom-call(s32[32,32]{1,0:T(8,128)} %bitcast.15, bf16[2,512,2816]{2,1,0:T(8,128)(2,1)} %bitcast.10, f32[1,2816]{1,0:T(1,128)} %bitcast.18, bf16[512,256]{1,0:T(8,128)(2,1)} %bitcast.22), custom_call_target="tpu_custom_call" | custom-call | flops 1476395008 | bytes 5767168 | tf_op jit(solution)/shard_map/coef/pallas_call | solution.py:89
  5.3 0.0 copy-start.4
  5.3 12.2 %all-to-all-start = ((bf16[32,88,256]{2,1,0:T(8,128)(2,1)}), bf16[32,88,256]{2,1,0:T(8,128)(2,1)S(1)}, u32[]{:S(2)}, u32[]{:S(2)}) async-start(bf16[32,88,256]{2,1,0:T(8,128)(2,1)} %coef.1), calls=%async_computation | async-start | bytes 2883584 | tf_op jit(solution)/shard_map/all_to_all | solution.py:362
  17.5 0.0 copy-done.6
  17.5 0.0 copy-done.10
  17.5 0.0 copy-start.9
  17.5 2.6 %copy-done.9 = bf16[1,2,512,2816]{3,2,1,0:T(8,128)(2,1)S(1)} copy-done((bf16[1,2,512,2816]{3,2,1,0:T(8,128)(2,1)S(1)}, bf16[1,2,512,2816]{3,2,1,0:T(8,128)(2,1)}, u32[]{:S(2)}) %copy-start.9) | copy-done | bytes 5767192
  20.1 8.0 %slot_rows.1 = (bf16[2,512,2816]{2,1,0:T(8,128)(2,1)S(1)}, bf16[2816,1024]{1,0:T(8,128)(2,1)S(1)}) custom-call(s32[32,32]{1,0:T(8,128)S(1)} %bitcast.16, bf16[2,512,2816]{2,1,0:T(8,128)(2,1)S(1)} %bitcast.20, f32[1,2816]{1,0:T(1,128)S(1)} %bitcast.21), custom_call_target="tpu_custom_call" | custom-call | flops 2214592512 | bytes 11534336 | tf_op jit(solution)/shard_map/slot_rows/pallas_call | solution.py:168
  28.2 2.5 %copy-done.2 = bf16[2,512,2816]{2,1,0:T(8,128)(2,1)} copy-done((bf16[2,512,2816]{2,1,0:T(8,128)(2,1)}, bf16[2,512,2816]{2,1,0:T(8,128)(2,1)S(1)}, u32[]{:S(2)}) %copy-start.2) | copy-done | bytes 5767192
  30.7 2.5 %copy-done.3 = bf16[2816,1024]{1,0:T(8,128)(2,1)} copy-done((bf16[2816,1024]{1,0:T(8,128)(2,1)}, bf16[2816,1024]{1,0:T(8,128)(2,1)S(1)}, u32[]{:S(2)}) %copy-start.3) | copy-done | bytes 5767192
  33.2 18.3 %all-to-all-done = bf16[32,88,256]{2,1,0:T(8,128)(2,1)S(1)} async-done(((bf16[32,88,256]{2,1,0:T(8,128)(2,1)}), bf16[32,88,256]{2,1,0:T(8,128)(2,1)S(1)}, u32[]{:S(2)}, u32[]{:S(2)}) %all-to-all-start) | async-done | bytes 1441824 | tf_op jit(solution)/shard_map/all_to_all | solution.py:362
  51.5 0.0 copy-done.4
  51.5 7.9 %residual.1 = bf16[2816,256]{1,0:T(8,128)(2,1)} custom-call(bf16[2816,256]{1,0:T(8,128)(2,1)S(1)} %bitcast.12, bf16[2,512,2816]{2,1,0:T(8,128)(2,1)} %copy-done.2, bf16[2816,1024]{1,0:T(8,128)(2,1)} %copy-done.3, bf16[512,256]{1,0:T(8,128)(2,1)S(1)} %bitcast.14), custom_call_target="tpu_custom_call" | custom-call | flops 2952790016 | bytes 2883584 | tf_op jit(solution)/shard_map/residual/pallas_call | solution.py:235
  59.4 7.6 %all-to-all-start.1 = ((bf16[32,88,256]{2,1,0:T(8,128)(2,1)}), bf16[32,88,256]{2,1,0:T(8,128)(2,1)S(1)}, u32[]{:S(2)}, u32[]{:S(2)}) async-start(bf16[32,88,256]{2,1,0:T(8,128)(2,1)} %bitcast.8), calls=%async_computation.1 | async-start | bytes 2883584 | tf_op jit(solution)/shard_map/all_to_all | solution.py:366
  67.0 0.0 copy-start
  67.0 2.6 %copy-done = bf16[1,2,512,2816]{3,2,1,0:T(8,128)(2,1)S(1)} copy-done((bf16[1,2,512,2816]{3,2,1,0:T(8,128)(2,1)S(1)}, bf16[1,2,512,2816]{3,2,1,0:T(8,128)(2,1)}, u32[]{:S(2)}) %copy-start) | copy-done | bytes 5767192
  69.6 7.0 %slot_cols.1.factor = bf16[2,512,2816]{2,1,0:T(8,128)(2,1)S(1)} custom-call(s32[32,32]{1,0:T(8,128)S(1)} %bitcast.17, bf16[2,512,2816]{2,1,0:T(8,128)(2,1)S(1)} %bitcast.11, f32[1,2816]{1,0:T(1,128)S(1)} %bitcast.19), custom_call_target="tpu_custom_call" | custom-call | flops 2214592512 | bytes 11534336 | tf_op jit(solution)/shard_map/slot_cols/pallas_call | solution.py:168
  76.7 0.0 copy-start.1
  76.7 2.5 %copy-done.1 = bf16[2,512,2816]{2,1,0:T(8,128)(2,1)} copy-done((bf16[2,512,2816]{2,1,0:T(8,128)(2,1)}, bf16[2,512,2816]{2,1,0:T(8,128)(2,1)S(1)}, u32[]{:S(2)}) %copy-start.1) | copy-done | bytes 5767192
  79.2 22.0 %all-to-all-done.1 = bf16[32,88,256]{2,1,0:T(8,128)(2,1)S(1)} async-done(((bf16[32,88,256]{2,1,0:T(8,128)(2,1)}), bf16[32,88,256]{2,1,0:T(8,128)(2,1)S(1)}, u32[]{:S(2)}, u32[]{:S(2)}) %all-to-all-start.1) | async-done | bytes 1441824 | tf_op jit(solution)/shard_map/all_to_all | solution.py:366
  101.2 3.8 %gradient.1 = bf16[8,32,512]{2,1,0:T(8,128)(2,1)S(1)} custom-call(bf16[2816,256]{1,0:T(8,128)(2,1)S(1)} %bitcast.13, bf16[2,512,2816]{2,1,0:T(8,128)(2,1)} %copy-done.1), custom_call_target="tpu_custom_call" | custom-call | flops 1476395008 | bytes 1441792 | tf_op jit(solution)/shard_map/gradient/pallas_call | solution.py:287
  104.9 14.1 %all_to_all.15.arrived = bf16[8,32,512]{2,1,0:T(8,128)(2,1)S(1)} all-to-all(bf16[8,32,512]{2,1,0:T(8,128)(2,1)S(1)} %gradient.1), channel_id=1, replica_groups=mesh['freq'=8,'tile'=32] {'freq'}, dimensions={0} | all-to-all | bytes 524288 | tf_op jit(solution)/shard_map/all_to_all | solution.py:368
  119.0 0.0 copy-done.8
  119.0 3.4 %to_time.1 = bf16[512,16,128]{2,1,0:T(8,128)(2,1)} custom-call(s32[512]{0:T(512)S(1)} %copy-done.8, bf16[8,32,512]{2,1,0:T(8,128)(2,1)S(1)} %all_to_all.15.arrived, bf16[256,256]{1,0:T(8,128)(2,1)S(1)} %copy-done.5), custom_call_target="tpu_custom_call" | custom-call | tf_op jit(solution)/shard_map/to_time/pallas_call | solution.py:336
  (9 shorter events, 0.0 us)
Async XLA Ops:
  0.0 17.5 %copy-start.6 = (s32[1,32,32]{2,1,0:T(8,128)S(1)}, s32[1,32,32]{2,1,0:T(8,128)}, u32[]{:S(2)}) copy-start(s32[1,32,32]{2,1,0:T(8,128)} %param.15) | copy-start | bytes 12292
  0.0 17.5 %copy-start.10 = (f32[1,1,2816]{2,1,0:T(1,128)S(1)}, f32[1,1,2816]{2,1,0:T(1,128)}, u32[]{:S(2)}) copy-start(f32[1,1,2816]{2,1,0:T(1,128)} %param.12) | copy-start | bytes 33796
  5.3 46.3 %copy-start.4 = (bf16[1,512,256]{2,1,0:T(8,128)(2,1)S(1)}, bf16[1,512,256]{2,1,0:T(8,128)(2,1)}, u32[]{:S(2)}) copy-start(bf16[1,512,256]{2,1,0:T(8,128)(2,1)} %param.10) | copy-start | bytes 786436
  5.3 46.2 %all-to-all-start = ((bf16[32,88,256]{2,1,0:T(8,128)(2,1)}), bf16[32,88,256]{2,1,0:T(8,128)(2,1)S(1)}, u32[]{:S(2)}, u32[]{:S(2)}) async-start(bf16[32,88,256]{2,1,0:T(8,128)(2,1)} %coef.1), calls=%async_computation | async-start | bytes 2883584 | tf_op jit(solution)/shard_map/all_to_all | solution.py:362
  17.5 2.6 %copy-start.9 = (bf16[1,2,512,2816]{3,2,1,0:T(8,128)(2,1)S(1)}, bf16[1,2,512,2816]{3,2,1,0:T(8,128)(2,1)}, u32[]{:S(2)}) copy-start(bf16[1,2,512,2816]{3,2,1,0:T(8,128)(2,1)} %param.11) | copy-start | bytes 17301508
  28.2 2.5 %copy-start.2 = (bf16[2,512,2816]{2,1,0:T(8,128)(2,1)}, bf16[2,512,2816]{2,1,0:T(8,128)(2,1)S(1)}, u32[]{:S(2)}) copy-start(bf16[2,512,2816]{2,1,0:T(8,128)(2,1)S(1)} %get-tuple-element.12.factor) | copy-start | bytes 17301508
  30.7 2.5 %copy-start.3 = (bf16[2816,1024]{1,0:T(8,128)(2,1)}, bf16[2816,1024]{1,0:T(8,128)(2,1)S(1)}, u32[]{:S(2)}) copy-start(bf16[2816,1024]{1,0:T(8,128)(2,1)S(1)} %get-tuple-element.13.turned) | copy-start | bytes 17301508
  51.5 15.5 %copy-start.7 = (f32[1,1,2816]{2,1,0:T(1,128)S(1)}, f32[1,1,2816]{2,1,0:T(1,128)}, u32[]{:S(2)}) copy-start(f32[1,1,2816]{2,1,0:T(1,128)} %param.14) | copy-start | bytes 33796
  59.4 41.8 %all-to-all-start.1 = ((bf16[32,88,256]{2,1,0:T(8,128)(2,1)}), bf16[32,88,256]{2,1,0:T(8,128)(2,1)S(1)}, u32[]{:S(2)}, u32[]{:S(2)}) async-start(bf16[32,88,256]{2,1,0:T(8,128)(2,1)} %bitcast.8), calls=%async_computation.1 | async-start | bytes 2883584 | tf_op jit(solution)/shard_map/all_to_all | solution.py:366
  67.0 2.6 %copy-start = (bf16[1,2,512,2816]{3,2,1,0:T(8,128)(2,1)S(1)}, bf16[1,2,512,2816]{3,2,1,0:T(8,128)(2,1)}, u32[]{:S(2)}) copy-start(bf16[1,2,512,2816]{3,2,1,0:T(8,128)(2,1)} %param.13) | copy-start | bytes 17301508
  76.7 2.5 %copy-start.1 = (bf16[2,512,2816]{2,1,0:T(8,128)(2,1)}, bf16[2,512,2816]{2,1,0:T(8,128)(2,1)S(1)}, u32[]{:S(2)}) copy-start(bf16[2,512,2816]{2,1,0:T(8,128)(2,1)S(1)} %slot_cols.1.factor) | copy-start | bytes 17301508
  79.2 39.9 %copy-start.5 = (bf16[256,256]{1,0:T(8,128)(2,1)S(1)}, bf16[256,256]{1,0:T(8,128)(2,1)}, u32[]{:S(2)}) copy-start(bf16[256,256]{1,0:T(8,128)(2,1)} %constant.2.clone.basis) | copy-start | bytes 393220
  79.2 39.9 %copy-start.8 = (s32[512]{0:T(512)S(1)}, s32[512]{0:T(512)}, u32[]{:S(2)}) copy-start(s32[512]{0:T(512)} %mute.1) | copy-start | bytes 6148

commit v3 on v2

--- a/solution.py
+++ b/solution.py
@@ -13,6 +13,7 @@
 NTIME = 128
 BLK = 256
 WIN = 384
+STAGGER_NS = 18000
 TIME_PIECES = 4
 OUT_PIECES = 4
 TURNED_PIECES = 2
@@ -76,6 +77,10 @@
             leaving[-1].start()
         for copy in leaving:
             copy.wait()
+
+        @pl.when(lax.axis_index("freq") % 2 == 1)
+        def _():
+            pl.delay(STAGGER_NS)
 
 
 def in_hbm(*arrays):

time: 123 us -> 111 us (0.902)
  waiting for transfers between devices: 40.4 us -> 16 us
  Pallas kernels: 35.3 us -> 53.3 us
  blocking collectives: 14.1 us -> 10.7 us
  starting transfers between devices: 19.8 us -> 18 us
    pallas_call x1, Pallas kernels: 5.25 us -> 23.3 us  [coef(): pl.pallas_call(coef_kernel, grid=(parts,), in_specs=[pl.BlockSpec(memory_...]
    all_to_all x1, waiting for transfers between devices: 18.3 us -> 5.07 us  [shards(): lax.all_to_all(sent, 'tile', split_axis=0, concat_axis=0, tiled=True)]
    all_to_all x1, waiting for transfers between devices: 22 us -> 10.9 us  [shards(): lax.all_to_all(back.reshape(tiles, RSLOT, width), 'tile', split_axis=0, c...]
    all_to_all x1, blocking collectives: 14.1 us -> 10.7 us  [shards(): lax.all_to_all(part, 'freq', split_axis=0, concat_axis=0, tiled=True)]
    all_to_all x1, starting transfers between devices: 7.58 us -> 5.88 us  [shards(): lax.all_to_all(back.reshape(tiles, RSLOT, width), 'tile', split_axis=0, c...]
  transfers between devices with their start and end apart: 2 -> 2, of which waited for: 2 -> 2; matrix products, arithmetic and copies ran while one was open for 0% -> 0% of each run, Pallas kernels for 12% -> 14%
where the time goes in v3:
time: 111 us
  Pallas kernels  53.3 us (48%)
  starting transfers between devices  18 us (16%)
  waiting for transfers between devices  16 us (14%)
  local copies, waits for them, and re-layouts  12.8 us (12%)
  blocking collectives  10.7 us (10%)
    pallas_call x1, Pallas kernels, coef(): pl.pallas_call(coef_kernel, grid=(parts,), in_specs=[pl.BlockSpec(memory_...  23.3 us
    pallas_call x2, Pallas kernels, slots(): pl.pallas_call(functools.partial(slot_kernel, by_row, with_turned), grid=...  15.1 us
    unnamed x22, local copies, waits for them, and re-layouts  12.8 us
    all_to_all x1, starting transfers between devices, shards(): lax.all_to_all(sent, 'tile', split_axis=0, concat_axis=0, tiled=True)  12.2 us
    all_to_all x1, waiting for transfers between devices, shards(): lax.all_to_all(back.reshape(tiles, RSLOT, width), 'tile', split_axis=0, c...  10.9 us
    all_to_all x1, blocking collectives, shards(): lax.all_to_all(part, 'freq', split_axis=0, concat_axis=0, tiled=True)  10.7 us
    pallas_call x1, Pallas kernels, residual(): pl.pallas_call(residual_kernel, grid=(parts,), in_specs=[pl.BlockSpec((ca...  7.86 us
    all_to_all x1, starting transfers between devices, shards(): lax.all_to_all(back.reshape(tiles, RSLOT, width), 'tile', split_axis=0, c...  5.88 us
  transfers between devices with their start and end apart: 2, of which 2 were waited for; matrix products, arithmetic and copies ran while one was open for 0% of the time, Pallas kernels for 14%

profile of v3, /device:TPU:1, one launch (start us, length us, event | category | flops | bytes accessed | tf_op | source)
XLA Modules:
  0.0 110.9 jit_solution(12069851384863393281)
XLA Ops:
  0.0 23.3 %coef.1 = bf16[32,88,256]{2,1,0:T(8,128)(2,1)} custom-call(s32[32,32]{1,0:T(8,128)} %bitcast.15, bf16[2,512,2816]{2,1,0:T(8,128)(2,1)} %bitcast.10, f32[1,2816]{1,0:T(1,128)} %bitcast.18, bf16[512,256]{1,0:T(8,128)(2,1)} %bitcast.22), custom_call_target="tpu_custom_call" | custom-call | flops 1476395008 | bytes 5767168 | tf_op jit(solution)/shard_map/coef/pallas_call | solution.py:94
  23.3 0.0 copy-start.4
  23.3 12.2 %all-to-all-start = ((bf16[32,88,256]{2,1,0:T(8,128)(2,1)}), bf16[32,88,256]{2,1,0:T(8,128)(2,1)S(1)}, u32[]{:S(2)}, u32[]{:S(2)}) async-start(bf16[32,88,256]{2,1,0:T(8,128)(2,1)} %coef.1), calls=%async_computation | async-start | bytes 2883584 | tf_op jit(solution)/shard_map/all_to_all | solution.py:367
  35.5 0.0 copy-done.6
  35.5 0.0 copy-done.10
  35.5 0.0 copy-start.9
  35.5 2.6 %copy-done.9 = bf16[1,2,512,2816]{3,2,1,0:T(8,128)(2,1)S(1)} copy-done((bf16[1,2,512,2816]{3,2,1,0:T(8,128)(2,1)S(1)}, bf16[1,2,512,2816]{3,2,1,0:T(8,128)(2,1)}, u32[]{:S(2)}) %copy-start.9) | copy-done | bytes 5767192
  38.1 8.0 %slot_rows.1 = (bf16[2,512,2816]{2,1,0:T(8,128)(2,1)S(1)}, bf16[2816,1024]{1,0:T(8,128)(2,1)S(1)}) custom-call(s32[32,32]{1,0:T(8,128)S(1)} %bitcast.16, bf16[2,512,2816]{2,1,0:T(8,128)(2,1)S(1)} %bitcast.20, f32[1,2816]{1,0:T(1,128)S(1)} %bitcast.21), custom_call_target="tpu_custom_call" | custom-call | flops 2214592512 | bytes 11534336 | tf_op jit(solution)/shard_map/slot_rows/pallas_call | solution.py:173
  46.2 0.0 copy-start.2
  46.2 2.5 %copy-done.2 = bf16[2,512,2816]{2,1,0:T(8,128)(2,1)} copy-done((bf16[2,512,2816]{2,1,0:T(8,128)(2,1)}, bf16[2,512,2816]{2,1,0:T(8,128)(2,1)S(1)}, u32[]{:S(2)}) %copy-start.2) | copy-done | bytes 5767192
  48.7 2.5 %copy-done.3 = bf16[2816,1024]{1,0:T(8,128)(2,1)} copy-done((bf16[2816,1024]{1,0:T(8,128)(2,1)}, bf16[2816,1024]{1,0:T(8,128)(2,1)S(1)}, u32[]{:S(2)}) %copy-start.3) | copy-done | bytes 5767192
  51.2 5.1 %all-to-all-done = bf16[32,88,256]{2,1,0:T(8,128)(2,1)S(1)} async-done(((bf16[32,88,256]{2,1,0:T(8,128)(2,1)}), bf16[32,88,256]{2,1,0:T(8,128)(2,1)S(1)}, u32[]{:S(2)}, u32[]{:S(2)}) %all-to-all-start) | async-done | bytes 1441824 | tf_op jit(solution)/shard_map/all_to_all | solution.py:367
  56.3 0.0 copy-done.4
  56.3 7.9 %residual.1 = bf16[2816,256]{1,0:T(8,128)(2,1)} custom-call(bf16[2816,256]{1,0:T(8,128)(2,1)S(1)} %bitcast.12, bf16[2,512,2816]{2,1,0:T(8,128)(2,1)} %copy-done.2, bf16[2816,1024]{1,0:T(8,128)(2,1)} %copy-done.3, bf16[512,256]{1,0:T(8,128)(2,1)S(1)} %bitcast.14), custom_call_target="tpu_custom_call" | custom-call | flops 2952790016 | bytes 2883584 | tf_op jit(solution)/shard_map/residual/pallas_call | solution.py:240
  64.1 5.9 %all-to-all-start.1 = ((bf16[32,88,256]{2,1,0:T(8,128)(2,1)}), bf16[32,88,256]{2,1,0:T(8,128)(2,1)S(1)}, u32[]{:S(2)}, u32[]{:S(2)}) async-start(bf16[32,88,256]{2,1,0:T(8,128)(2,1)} %bitcast.8), calls=%async_computation.1 | async-start | bytes 2883584 | tf_op jit(solution)/shard_map/all_to_all | solution.py:371
  70.0 0.0 copy-start
  70.0 2.6 %copy-done = bf16[1,2,512,2816]{3,2,1,0:T(8,128)(2,1)S(1)} copy-done((bf16[1,2,512,2816]{3,2,1,0:T(8,128)(2,1)S(1)}, bf16[1,2,512,2816]{3,2,1,0:T(8,128)(2,1)}, u32[]{:S(2)}) %copy-start) | copy-done | bytes 5767192
  72.7 7.0 %slot_cols.1.factor = bf16[2,512,2816]{2,1,0:T(8,128)(2,1)S(1)} custom-call(s32[32,32]{1,0:T(8,128)S(1)} %bitcast.17, bf16[2,512,2816]{2,1,0:T(8,128)(2,1)S(1)} %bitcast.11, f32[1,2816]{1,0:T(1,128)S(1)} %bitcast.19), custom_call_target="tpu_custom_call" | custom-call | flops 2214592512 | bytes 11534336 | tf_op jit(solution)/shard_map/slot_cols/pallas_call | solution.py:173
  79.7 0.0 copy-start.1
  79.7 2.5 %copy-done.1 = bf16[2,512,2816]{2,1,0:T(8,128)(2,1)} copy-done((bf16[2,512,2816]{2,1,0:T(8,128)(2,1)}, bf16[2,512,2816]{2,1,0:T(8,128)(2,1)S(1)}, u32[]{:S(2)}) %copy-start.1) | copy-done | bytes 5767192
  82.2 10.9 %all-to-all-done.1 = bf16[32,88,256]{2,1,0:T(8,128)(2,1)S(1)} async-done(((bf16[32,88,256]{2,1,0:T(8,128)(2,1)}), bf16[32,88,256]{2,1,0:T(8,128)(2,1)S(1)}, u32[]{:S(2)}, u32[]{:S(2)}) %all-to-all-start.1) | async-done | bytes 1441824 | tf_op jit(solution)/shard_map/all_to_all | solution.py:371
  93.1 3.8 %gradient.1 = bf16[8,32,512]{2,1,0:T(8,128)(2,1)S(1)} custom-call(bf16[2816,256]{1,0:T(8,128)(2,1)S(1)} %bitcast.13, bf16[2,512,2816]{2,1,0:T(8,128)(2,1)} %copy-done.1), custom_call_target="tpu_custom_call" | custom-call | flops 1476395008 | bytes 1441792 | tf_op jit(solution)/shard_map/gradient/pallas_call | solution.py:292
  96.9 10.7 %all_to_all.15.arrived = bf16[8,32,512]{2,1,0:T(8,128)(2,1)S(1)} all-to-all(bf16[8,32,512]{2,1,0:T(8,128)(2,1)S(1)} %gradient.1), channel_id=1, replica_groups=mesh['freq'=8,'tile'=32] {'freq'}, dimensions={0} | all-to-all | bytes 524288 | tf_op jit(solution)/shard_map/all_to_all | solution.py:373
  107.5 3.4 %to_time.1 = bf16[512,16,128]{2,1,0:T(8,128)(2,1)} custom-call(s32[512]{0:T(512)S(1)} %copy-done.8, bf16[8,32,512]{2,1,0:T(8,128)(2,1)S(1)} %all_to_all.15.arrived, bf16[256,256]{1,0:T(8,128)(2,1)S(1)} %copy-done.5), custom_call_target="tpu_custom_call" | custom-call | tf_op jit(solution)/shard_map/to_time/pallas_call | solution.py:341
  (9 shorter events, 0.0 us)
Async XLA Ops:
  0.0 35.5 %copy-start.6 = (s32[1,32,32]{2,1,0:T(8,128)S(1)}, s32[1,32,32]{2,1,0:T(8,128)}, u32[]{:S(2)}) copy-start(s32[1,32,32]{2,1,0:T(8,128)} %param.15) | copy-start | bytes 12292
  0.0 35.5 %copy-start.10 = (f32[1,1,2816]{2,1,0:T(1,128)S(1)}, f32[1,1,2816]{2,1,0:T(1,128)}, u32[]{:S(2)}) copy-start(f32[1,1,2816]{2,1,0:T(1,128)} %param.12) | copy-start | bytes 33796
  23.3 33.0 %copy-start.4 = (bf16[1,512,256]{2,1,0:T(8,128)(2,1)S(1)}, bf16[1,512,256]{2,1,0:T(8,128)(2,1)}, u32[]{:S(2)}) copy-start(bf16[1,512,256]{2,1,0:T(8,128)(2,1)} %param.10) | copy-start | bytes 786436
  23.3 33.0 %all-to-all-start = ((bf16[32,88,256]{2,1,0:T(8,128)(2,1)}), bf16[32,88,256]{2,1,0:T(8,128)(2,1)S(1)}, u32[]{:S(2)}, u32[]{:S(2)}) async-start(bf16[32,88,256]{2,1,0:T(8,128)(2,1)} %coef.1), calls=%async_computation | async-start | bytes 2883584 | tf_op jit(solution)/shard_map/all_to_all | solution.py:367
  35.5 2.6 %copy-start.9 = (bf16[1,2,512,2816]{3,2,1,0:T(8,128)(2,1)S(1)}, bf16[1,2,512,2816]{3,2,1,0:T(8,128)(2,1)}, u32[]{:S(2)}) copy-start(bf16[1,2,512,2816]{3,2,1,0:T(8,128)(2,1)} %param.11) | copy-start | bytes 17301508
  46.2 2.5 %copy-start.2 = (bf16[2,512,2816]{2,1,0:T(8,128)(2,1)}, bf16[2,512,2816]{2,1,0:T(8,128)(2,1)S(1)}, u32[]{:S(2)}) copy-start(bf16[2,512,2816]{2,1,0:T(8,128)(2,1)S(1)} %get-tuple-element.12.factor) | copy-start | bytes 17301508
  48.7 2.5 %copy-start.3 = (bf16[2816,1024]{1,0:T(8,128)(2,1)}, bf16[2816,1024]{1,0:T(8,128)(2,1)S(1)}, u32[]{:S(2)}) copy-start(bf16[2816,1024]{1,0:T(8,128)(2,1)S(1)} %get-tuple-element.13.turned) | copy-start | bytes 17301508
  56.3 13.8 %copy-start.7 = (f32[1,1,2816]{2,1,0:T(1,128)S(1)}, f32[1,1,2816]{2,1,0:T(1,128)}, u32[]{:S(2)}) copy-start(f32[1,1,2816]{2,1,0:T(1,128)} %param.14) | copy-start | bytes 33796
  64.1 29.0 %all-to-all-start.1 = ((bf16[32,88,256]{2,1,0:T(8,128)(2,1)}), bf16[32,88,256]{2,1,0:T(8,128)(2,1)S(1)}, u32[]{:S(2)}, u32[]{:S(2)}) async-start(bf16[32,88,256]{2,1,0:T(8,128)(2,1)} %bitcast.8), calls=%async_computation.1 | async-start | bytes 2883584 | tf_op jit(solution)/shard_map/all_to_all | solution.py:371
  70.0 2.6 %copy-start = (bf16[1,2,512,2816]{3,2,1,0:T(8,128)(2,1)S(1)}, bf16[1,2,512,2816]{3,2,1,0:T(8,128)(2,1)}, u32[]{:S(2)}) copy-start(bf16[1,2,512,2816]{3,2,1,0:T(8,128)(2,1)} %param.13) | copy-start | bytes 17301508
  79.7 2.5 %copy-start.1 = (bf16[2,512,2816]{2,1,0:T(8,128)(2,1)}, bf16[2,512,2816]{2,1,0:T(8,128)(2,1)S(1)}, u32[]{:S(2)}) copy-start(bf16[2,512,2816]{2,1,0:T(8,128)(2,1)S(1)} %slot_cols.1.factor) | copy-start | bytes 17301508
  82.2 25.3 %copy-start.5 = (bf16[256,256]{1,0:T(8,128)(2,1)S(1)}, bf16[256,256]{1,0:T(8,128)(2,1)}, u32[]{:S(2)}) copy-start(bf16[256,256]{1,0:T(8,128)(2,1)} %constant.2.clone.basis) | copy-start | bytes 393220
  82.2 25.3 %copy-start.8 = (s32[512]{0:T(512)S(1)}, s32[512]{0:T(512)}, u32[]{:S(2)}) copy-start(s32[512]{0:T(512)} %mute.1) | copy-start | bytes 6148

commit v4 on v3

--- a/solution.py
+++ b/solution.py
@@ -14,9 +14,9 @@
 BLK = 256
 WIN = 384
 STAGGER_NS = 18000
-TIME_PIECES = 4
+TIME_PIECES = 8
 OUT_PIECES = 4
-TURNED_PIECES = 2
+TURNED_SIXTEENTHS = (8,)
 F32 = jnp.float32
 BF16 = jnp.bfloat16
 NT_DIMS = (((1,), (1,)), ((), ()))
@@ -195,15 +195,23 @@
     return stacked[:rows] + swapped * sign
 
 
+def piece_spans(total):
+    spans, first = [], 0
+    for part in TURNED_SIXTEENTHS:
+        spans.append((first, total // 176 * 11 * part))
+        first += spans[-1][1]
+    return spans + [(first, total - first)]
+
+
 def residual_kernel(coefs, factor, turned, data, out, held, real, both, ready, sems, out_sems):
     part = pl.program_id(0)
     _, rows, cap = factor.shape
     lanes = coefs.shape[1]
     half = lanes // 2
-    step = cap // TURNED_PIECES
+    spans = piece_spans(cap)
     copies = []
-    for k in range(TURNED_PIECES):
-        at = pl.ds(k * step, step)
+    for k, (first, size) in enumerate(spans):
+        at = pl.ds(first, size)
         copies.append(pltpu.make_async_copy(turned.at[at], held.at[at], sems.at[k]))
 
     @pl.when(part == 0)
@@ -223,9 +231,9 @@
         both[rows:] = (swapped * jnp.where(side, 1.0, -1.0)).astype(BF16)
         leaving = []
         weights = both[...]
-        for k in range(TURNED_PIECES):
+        for k, (first, size) in enumerate(spans):
             copies[k].wait()
-            at = slice(k * step, k * step + step)
+            at = slice(first, first + size)
             ready[at] = jnp.dot(held[at], weights, preferred_element_type=F32).astype(BF16)
             leaving.append(pltpu.make_async_copy(ready.at[at], out.at[at], out_sems.at[k]))
             leaving[-1].start()
@@ -253,8 +261,8 @@
             pltpu.VMEM((rows, lanes), F32),
             pltpu.VMEM((parts * rows, lanes), BF16),
             pltpu.VMEM((cap, lanes), BF16),
-            pltpu.SemaphoreType.DMA((TURNED_PIECES,)),
-            pltpu.SemaphoreType.DMA((TURNED_PIECES,)),
+            pltpu.SemaphoreType.DMA((len(TURNED_SIXTEENTHS) + 1,)),
+            pltpu.SemaphoreType.DMA((len(TURNED_SIXTEENTHS) + 1,)),
         ],
         compiler_params=pltpu.CompilerParams(vmem_limit_bytes=32 << 20),
         cost_estimate=pl.CostEstimate(flops=8 * cap * rows * lanes, bytes_accessed=2 * cap * lanes * 2, transcendentals=0),
@@ -332,8 +340,10 @@
         leaving(step).wait()
         return carry
 
-    lax.fori_loop(0, sems.shape[0], push, 0)
-    lax.fori_loop(0, sems.shape[0], finish, 0)
+    for step in range(sems.shape[0]):
+        push(step, 0)
+    for step in range(sems.shape[0]):
+        finish(step, 0)
 
 
 def to_time(mute, arrived, basis, rows, share):

time: 111 us -> 111 us (level)
  no operation moved by 1% of the time
where the time goes in v4:
time: 111 us; the launch traced here: 110 us
  Pallas kernels  52.7 us (47%)
  starting transfers between devices  18 us (16%)
  waiting for transfers between devices  16 us (14%)
  local copies, waits for them, and re-layouts  12.8 us (12%)
  blocking collectives  10.7 us (10%)
    pallas_call x1, Pallas kernels, coef(): pl.pallas_call(coef_kernel, grid=(parts,), in_specs=[pl.BlockSpec(memory_...  23.3 us
    pallas_call x2, Pallas kernels, slots(): pl.pallas_call(functools.partial(slot_kernel, by_row, with_turned), grid=...  15.1 us
    unnamed x22, local copies, waits for them, and re-layouts  12.8 us
    all_to_all x1, starting transfers between devices, shards(): lax.all_to_all(sent, 'tile', split_axis=0, concat_axis=0, tiled=True)  12.2 us
    all_to_all x1, waiting for transfers between devices, shards(): lax.all_to_all(back.reshape(tiles, RSLOT, width), 'tile', split_axis=0, c...  10.9 us
    all_to_all x1, blocking collectives, shards(): lax.all_to_all(part, 'freq', split_axis=0, concat_axis=0, tiled=True)  10.7 us
    pallas_call x1, Pallas kernels, residual(): pl.pallas_call(residual_kernel, grid=(parts,), in_specs=[pl.BlockSpec((ca...  7.86 us
    all_to_all x1, starting transfers between devices, shards(): lax.all_to_all(back.reshape(tiles, RSLOT, width), 'tile', split_axis=0, c...  5.88 us
  transfers between devices with their start and end apart: 2, of which 2 were waited for; matrix products, arithmetic and copies ran while one was open for 0% of the time, Pallas kernels for 14%

profile of v4, /device:TPU:1, one launch (start us, length us, event | category | flops | bytes accessed | tf_op | source)
XLA Modules:
  0.0 110.3 jit_solution(17631436083712701972)
XLA Ops:
  0.0 23.3 %coef.1 = bf16[32,88,256]{2,1,0:T(8,128)(2,1)} custom-call(s32[32,32]{1,0:T(8,128)} %bitcast.15, bf16[2,512,2816]{2,1,0:T(8,128)(2,1)} %bitcast.10, f32[1,2816]{1,0:T(1,128)} %bitcast.18, bf16[512,256]{1,0:T(8,128)(2,1)} %bitcast.22), custom_call_target="tpu_custom_call" | custom-call | flops 1476395008 | bytes 5767168 | tf_op jit(solution)/shard_map/coef/pallas_call | solution.py:94
  23.3 0.0 copy-start.4
  23.3 12.2 %all-to-all-start = ((bf16[32,88,256]{2,1,0:T(8,128)(2,1)}), bf16[32,88,256]{2,1,0:T(8,128)(2,1)S(1)}, u32[]{:S(2)}, u32[]{:S(2)}) async-start(bf16[32,88,256]{2,1,0:T(8,128)(2,1)} %coef.1), calls=%async_computation | async-start | bytes 2883584 | tf_op jit(solution)/shard_map/all_to_all | solution.py:377
  35.5 0.0 copy-done.6
  35.5 0.0 copy-done.10
  35.5 0.0 copy-start.9
  35.5 2.6 %copy-done.9 = bf16[1,2,512,2816]{3,2,1,0:T(8,128)(2,1)S(1)} copy-done((bf16[1,2,512,2816]{3,2,1,0:T(8,128)(2,1)S(1)}, bf16[1,2,512,2816]{3,2,1,0:T(8,128)(2,1)}, u32[]{:S(2)}) %copy-start.9) | copy-done | bytes 5767192
  38.1 8.0 %slot_rows.1 = (bf16[2,512,2816]{2,1,0:T(8,128)(2,1)S(1)}, bf16[2816,1024]{1,0:T(8,128)(2,1)S(1)}) custom-call(s32[32,32]{1,0:T(8,128)S(1)} %bitcast.16, bf16[2,512,2816]{2,1,0:T(8,128)(2,1)S(1)} %bitcast.20, f32[1,2816]{1,0:T(1,128)S(1)} %bitcast.21), custom_call_target="tpu_custom_call" | custom-call | flops 2214592512 | bytes 11534336 | tf_op jit(solution)/shard_map/slot_rows/pallas_call | solution.py:173
  46.2 0.0 copy-start.2
  46.2 2.5 %copy-done.2 = bf16[2,512,2816]{2,1,0:T(8,128)(2,1)} copy-done((bf16[2,512,2816]{2,1,0:T(8,128)(2,1)}, bf16[2,512,2816]{2,1,0:T(8,128)(2,1)S(1)}, u32[]{:S(2)}) %copy-start.2) | copy-done | bytes 5767192
  48.7 2.5 %copy-done.3 = bf16[2816,1024]{1,0:T(8,128)(2,1)} copy-done((bf16[2816,1024]{1,0:T(8,128)(2,1)}, bf16[2816,1024]{1,0:T(8,128)(2,1)S(1)}, u32[]{:S(2)}) %copy-start.3) | copy-done | bytes 5767192
  51.2 5.1 %all-to-all-done = bf16[32,88,256]{2,1,0:T(8,128)(2,1)S(1)} async-done(((bf16[32,88,256]{2,1,0:T(8,128)(2,1)}), bf16[32,88,256]{2,1,0:T(8,128)(2,1)S(1)}, u32[]{:S(2)}, u32[]{:S(2)}) %all-to-all-start) | async-done | bytes 1441824 | tf_op jit(solution)/shard_map/all_to_all | solution.py:377
  56.3 0.0 copy-done.4
  56.3 7.9 %residual.1 = bf16[2816,256]{1,0:T(8,128)(2,1)} custom-call(bf16[2816,256]{1,0:T(8,128)(2,1)S(1)} %bitcast.12, bf16[2,512,2816]{2,1,0:T(8,128)(2,1)} %copy-done.2, bf16[2816,1024]{1,0:T(8,128)(2,1)} %copy-done.3, bf16[512,256]{1,0:T(8,128)(2,1)S(1)} %bitcast.14), custom_call_target="tpu_custom_call" | custom-call | flops 2952790016 | bytes 2883584 | tf_op jit(solution)/shard_map/residual/pallas_call | solution.py:248
  64.1 5.9 %all-to-all-start.1 = ((bf16[32,88,256]{2,1,0:T(8,128)(2,1)}), bf16[32,88,256]{2,1,0:T(8,128)(2,1)S(1)}, u32[]{:S(2)}, u32[]{:S(2)}) async-start(bf16[32,88,256]{2,1,0:T(8,128)(2,1)} %bitcast.8), calls=%async_computation.1 | async-start | bytes 2883584 | tf_op jit(solution)/shard_map/all_to_all | solution.py:381
  70.0 0.0 copy-start
  70.0 2.6 %copy-done = bf16[1,2,512,2816]{3,2,1,0:T(8,128)(2,1)S(1)} copy-done((bf16[1,2,512,2816]{3,2,1,0:T(8,128)(2,1)S(1)}, bf16[1,2,512,2816]{3,2,1,0:T(8,128)(2,1)}, u32[]{:S(2)}) %copy-start) | copy-done | bytes 5767192
  72.7 7.0 %slot_cols.1.factor = bf16[2,512,2816]{2,1,0:T(8,128)(2,1)S(1)} custom-call(s32[32,32]{1,0:T(8,128)S(1)} %bitcast.17, bf16[2,512,2816]{2,1,0:T(8,128)(2,1)S(1)} %bitcast.11, f32[1,2816]{1,0:T(1,128)S(1)} %bitcast.19), custom_call_target="tpu_custom_call" | custom-call | flops 2214592512 | bytes 11534336 | tf_op jit(solution)/shard_map/slot_cols/pallas_call | solution.py:173
  79.7 2.5 %copy-done.1 = bf16[2,512,2816]{2,1,0:T(8,128)(2,1)} copy-done((bf16[2,512,2816]{2,1,0:T(8,128)(2,1)}, bf16[2,512,2816]{2,1,0:T(8,128)(2,1)S(1)}, u32[]{:S(2)}) %copy-start.1) | copy-done | bytes 5767192
  82.2 10.9 %all-to-all-done.1 = bf16[32,88,256]{2,1,0:T(8,128)(2,1)S(1)} async-done(((bf16[32,88,256]{2,1,0:T(8,128)(2,1)}), bf16[32,88,256]{2,1,0:T(8,128)(2,1)S(1)}, u32[]{:S(2)}, u32[]{:S(2)}) %all-to-all-start.1) | async-done | bytes 1441824 | tf_op jit(solution)/shard_map/all_to_all | solution.py:381
  93.1 3.8 %gradient.1 = bf16[8,32,512]{2,1,0:T(8,128)(2,1)S(1)} custom-call(bf16[2816,256]{1,0:T(8,128)(2,1)S(1)} %bitcast.13, bf16[2,512,2816]{2,1,0:T(8,128)(2,1)} %copy-done.1), custom_call_target="tpu_custom_call" | custom-call | flops 1476395008 | bytes 1441792 | tf_op jit(solution)/shard_map/gradient/pallas_call | solution.py:300
  96.9 10.7 %all_to_all.15.arrived = bf16[8,32,512]{2,1,0:T(8,128)(2,1)S(1)} all-to-all(bf16[8,32,512]{2,1,0:T(8,128)(2,1)S(1)} %gradient.1), channel_id=1, replica_groups=mesh['freq'=8,'tile'=32] {'freq'}, dimensions={0} | all-to-all | bytes 524288 | tf_op jit(solution)/shard_map/all_to_all | solution.py:383
  107.5 0.0 copy-done.5
  107.5 2.7 %to_time.1 = bf16[512,16,128]{2,1,0:T(8,128)(2,1)} custom-call(s32[512]{0:T(512)S(1)} %copy-done.8, bf16[8,32,512]{2,1,0:T(8,128)(2,1)S(1)} %all_to_all.15.arrived, bf16[256,256]{1,0:T(8,128)(2,1)S(1)} %copy-done.5), custom_call_target="tpu_custom_call" | custom-call | tf_op jit(solution)/shard_map/to_time/pallas_call | solution.py:351
  (9 shorter events, 0.0 us)
Async XLA Ops:
  0.0 35.5 %copy-start.6 = (s32[1,32,32]{2,1,0:T(8,128)S(1)}, s32[1,32,32]{2,1,0:T(8,128)}, u32[]{:S(2)}) copy-start(s32[1,32,32]{2,1,0:T(8,128)} %param.15) | copy-start | bytes 12292
  0.0 35.5 %copy-start.10 = (f32[1,1,2816]{2,1,0:T(1,128)S(1)}, f32[1,1,2816]{2,1,0:T(1,128)}, u32[]{:S(2)}) copy-start(f32[1,1,2816]{2,1,0:T(1,128)} %param.12) | copy-start | bytes 33796
  23.3 33.0 %copy-start.4 = (bf16[1,512,256]{2,1,0:T(8,128)(2,1)S(1)}, bf16[1,512,256]{2,1,0:T(8,128)(2,1)}, u32[]{:S(2)}) copy-start(bf16[1,512,256]{2,1,0:T(8,128)(2,1)} %param.10) | copy-start | bytes 786436
  23.3 33.0 %all-to-all-start = ((bf16[32,88,256]{2,1,0:T(8,128)(2,1)}), bf16[32,88,256]{2,1,0:T(8,128)(2,1)S(1)}, u32[]{:S(2)}, u32[]{:S(2)}) async-start(bf16[32,88,256]{2,1,0:T(8,128)(2,1)} %coef.1), calls=%async_computation | async-start | bytes 2883584 | tf_op jit(solution)/shard_map/all_to_all | solution.py:377
  35.5 2.6 %copy-start.9 = (bf16[1,2,512,2816]{3,2,1,0:T(8,128)(2,1)S(1)}, bf16[1,2,512,2816]{3,2,1,0:T(8,128)(2,1)}, u32[]{:S(2)}) copy-start(bf16[1,2,512,2816]{3,2,1,0:T(8,128)(2,1)} %param.11) | copy-start | bytes 17301508
  46.2 2.5 %copy-start.2 = (bf16[2,512,2816]{2,1,0:T(8,128)(2,1)}, bf16[2,512,2816]{2,1,0:T(8,128)(2,1)S(1)}, u32[]{:S(2)}) copy-start(bf16[2,512,2816]{2,1,0:T(8,128)(2,1)S(1)} %get-tuple-element.12.factor) | copy-start | bytes 17301508
  48.7 2.5 %copy-start.3 = (bf16[2816,1024]{1,0:T(8,128)(2,1)}, bf16[2816,1024]{1,0:T(8,128)(2,1)S(1)}, u32[]{:S(2)}) copy-start(bf16[2816,1024]{1,0:T(8,128)(2,1)S(1)} %get-tuple-element.13.turned) | copy-start | bytes 17301508
  56.3 13.8 %copy-start.7 = (f32[1,1,2816]{2,1,0:T(1,128)S(1)}, f32[1,1,2816]{2,1,0:T(1,128)}, u32[]{:S(2)}) copy-start(f32[1,1,2816]{2,1,0:T(1,128)} %param.14) | copy-start | bytes 33796
  64.1 29.0 %all-to-all-start.1 = ((bf16[32,88,256]{2,1,0:T(8,128)(2,1)}), bf16[32,88,256]{2,1,0:T(8,128)(2,1)S(1)}, u32[]{:S(2)}, u32[]{:S(2)}) async-start(bf16[32,88,256]{2,1,0:T(8,128)(2,1)} %bitcast.8), calls=%async_computation.1 | async-start | bytes 2883584 | tf_op jit(solution)/shard_map/all_to_all | solution.py:381
  70.0 2.6 %copy-start = (bf16[1,2,512,2816]{3,2,1,0:T(8,128)(2,1)S(1)}, bf16[1,2,512,2816]{3,2,1,0:T(8,128)(2,1)}, u32[]{:S(2)}) copy-start(bf16[1,2,512,2816]{3,2,1,0:T(8,128)(2,1)} %param.13) | copy-start | bytes 17301508
  79.7 2.5 %copy-start.1 = (bf16[2,512,2816]{2,1,0:T(8,128)(2,1)}, bf16[2,512,2816]{2,1,0:T(8,128)(2,1)S(1)}, u32[]{:S(2)}) copy-start(bf16[2,512,2816]{2,1,0:T(8,128)(2,1)S(1)} %slot_cols.1.factor) | copy-start | bytes 17301508
  82.2 25.3 %copy-start.5 = (bf16[256,256]{1,0:T(8,128)(2,1)S(1)}, bf16[256,256]{1,0:T(8,128)(2,1)}, u32[]{:S(2)}) copy-start(bf16[256,256]{1,0:T(8,128)(2,1)} %constant.2.clone.basis) | copy-start | bytes 393220
  82.2 25.3 %copy-start.8 = (s32[512]{0:T(512)S(1)}, s32[512]{0:T(512)}, u32[]{:S(2)}) copy-start(s32[512]{0:T(512)} %mute.1) | copy-start | bytes 6148

commit v5 on v4

--- a/solution.py
+++ b/solution.py
@@ -13,7 +13,7 @@
 NTIME = 128
 BLK = 256
 WIN = 384
-STAGGER_NS = 18000
+STAGGER_NS = 17500
 TIME_PIECES = 8
 OUT_PIECES = 4
 TURNED_SIXTEENTHS = (8,)
@@ -235,8 +235,10 @@
             copies[k].wait()
             at = slice(first, first + size)
             ready[at] = jnp.dot(held[at], weights, preferred_element_type=F32).astype(BF16)
-            leaving.append(pltpu.make_async_copy(ready.at[at], out.at[at], out_sems.at[k]))
-            leaving[-1].start()
+            for part_of in range(2):
+                at = slice(first + part_of * size // 2, first + (part_of + 1) * size // 2)
+                leaving.append(pltpu.make_async_copy(ready.at[at], out.at[at], out_sems.at[2 * k + part_of]))
+                leaving[-1].start()
         for copy in leaving:
             copy.wait()
 
@@ -262,7 +264,7 @@
             pltpu.VMEM((parts * rows, lanes), BF16),
             pltpu.VMEM((cap, lanes), BF16),
             pltpu.SemaphoreType.DMA((len(TURNED_SIXTEENTHS) + 1,)),
-            pltpu.SemaphoreType.DMA((len(TURNED_SIXTEENTHS) + 1,)),
+            pltpu.SemaphoreType.DMA((2 * len(TURNED_SIXTEENTHS) + 2,)),
         ],
         compiler_params=pltpu.CompilerParams(vmem_limit_bytes=32 << 20),
         cost_estimate=pl.CostEstimate(flops=8 * cap * rows * lanes, bytes_accessed=2 * cap * lanes * 2, transcendentals=0),

time: 111 us -> 110 us (level)
  no operation moved by 1% of the time
where the time goes in v5:
time: 110 us
  Pallas kernels  52.2 us (47%)
  starting transfers between devices  18.4 us (17%)
  waiting for transfers between devices  15.9 us (14%)
  local copies, waits for them, and re-layouts  12.8 us (12%)
  blocking collectives  10.7 us (10%)
    pallas_call x1, Pallas kernels, coef(): pl.pallas_call(coef_kernel, grid=(parts,), in_specs=[pl.BlockSpec(memory_...  22.8 us
    pallas_call x2, Pallas kernels, slots(): pl.pallas_call(functools.partial(slot_kernel, by_row, with_turned), grid=...  15.1 us
    unnamed x22, local copies, waits for them, and re-layouts  12.8 us
    all_to_all x1, starting transfers between devices, shards(): lax.all_to_all(sent, 'tile', split_axis=0, concat_axis=0, tiled=True)  12.2 us
    all_to_all x1, waiting for transfers between devices, shards(): lax.all_to_all(back.reshape(tiles, RSLOT, width), 'tile', split_axis=0, c...  10.8 us
    all_to_all x1, blocking collectives, shards(): lax.all_to_all(part, 'freq', split_axis=0, concat_axis=0, tiled=True)  10.7 us
    pallas_call x1, Pallas kernels, residual(): pl.pallas_call(residual_kernel, grid=(parts,), in_specs=[pl.BlockSpec((ca...  7.87 us
    all_to_all x1, starting transfers between devices, shards(): lax.all_to_all(back.reshape(tiles, RSLOT, width), 'tile', split_axis=0, c...  6.19 us
  transfers between devices with their start and end apart: 2, of which 2 were waited for; matrix products, arithmetic and copies ran while one was open for 0% of the time, Pallas kernels for 14%

profile of v5, /device:TPU:1, one launch (start us, length us, event | category | flops | bytes accessed | tf_op | source)
XLA Modules:
  0.0 110.1 jit_solution(4547693625118609347)
XLA Ops:
  0.0 22.8 %coef.1 = bf16[32,88,256]{2,1,0:T(8,128)(2,1)} custom-call(s32[32,32]{1,0:T(8,128)} %bitcast.15, bf16[2,512,2816]{2,1,0:T(8,128)(2,1)} %bitcast.10, f32[1,2816]{1,0:T(1,128)} %bitcast.18, bf16[512,256]{1,0:T(8,128)(2,1)} %bitcast.22), custom_call_target="tpu_custom_call" | custom-call | flops 1476395008 | bytes 5767168 | tf_op jit(solution)/shard_map/coef/pallas_call | solution.py:94
  22.8 0.0 copy-start.4
  22.8 12.2 %all-to-all-start = ((bf16[32,88,256]{2,1,0:T(8,128)(2,1)}), bf16[32,88,256]{2,1,0:T(8,128)(2,1)S(1)}, u32[]{:S(2)}, u32[]{:S(2)}) async-start(bf16[32,88,256]{2,1,0:T(8,128)(2,1)} %coef.1), calls=%async_computation | async-start | bytes 2883584 | tf_op jit(solution)/shard_map/all_to_all | solution.py:379
  35.0 0.0 copy-done.6
  35.0 0.0 copy-done.10
  35.0 0.0 copy-start.9
  35.0 2.6 %copy-done.9 = bf16[1,2,512,2816]{3,2,1,0:T(8,128)(2,1)S(1)} copy-done((bf16[1,2,512,2816]{3,2,1,0:T(8,128)(2,1)S(1)}, bf16[1,2,512,2816]{3,2,1,0:T(8,128)(2,1)}, u32[]{:S(2)}) %copy-start.9) | copy-done | bytes 5767192
  37.6 8.0 %slot_rows.1 = (bf16[2,512,2816]{2,1,0:T(8,128)(2,1)S(1)}, bf16[2816,1024]{1,0:T(8,128)(2,1)S(1)}) custom-call(s32[32,32]{1,0:T(8,128)S(1)} %bitcast.16, bf16[2,512,2816]{2,1,0:T(8,128)(2,1)S(1)} %bitcast.20, f32[1,2816]{1,0:T(1,128)S(1)} %bitcast.21), custom_call_target="tpu_custom_call" | custom-call | flops 2214592512 | bytes 11534336 | tf_op jit(solution)/shard_map/slot_rows/pallas_call | solution.py:173
  45.7 0.0 copy-start.2
  45.7 2.5 %copy-done.2 = bf16[2,512,2816]{2,1,0:T(8,128)(2,1)} copy-done((bf16[2,512,2816]{2,1,0:T(8,128)(2,1)}, bf16[2,512,2816]{2,1,0:T(8,128)(2,1)S(1)}, u32[]{:S(2)}) %copy-start.2) | copy-done | bytes 5767192
  48.2 2.5 %copy-done.3 = bf16[2816,1024]{1,0:T(8,128)(2,1)} copy-done((bf16[2816,1024]{1,0:T(8,128)(2,1)}, bf16[2816,1024]{1,0:T(8,128)(2,1)S(1)}, u32[]{:S(2)}) %copy-start.3) | copy-done | bytes 5767192
  50.7 5.1 %all-to-all-done = bf16[32,88,256]{2,1,0:T(8,128)(2,1)S(1)} async-done(((bf16[32,88,256]{2,1,0:T(8,128)(2,1)}), bf16[32,88,256]{2,1,0:T(8,128)(2,1)S(1)}, u32[]{:S(2)}, u32[]{:S(2)}) %all-to-all-start) | async-done | bytes 1441824 | tf_op jit(solution)/shard_map/all_to_all | solution.py:379
  55.8 0.0 copy-done.4
  55.8 7.9 %residual.1 = bf16[2816,256]{1,0:T(8,128)(2,1)} custom-call(bf16[2816,256]{1,0:T(8,128)(2,1)S(1)} %bitcast.12, bf16[2,512,2816]{2,1,0:T(8,128)(2,1)} %copy-done.2, bf16[2816,1024]{1,0:T(8,128)(2,1)} %copy-done.3, bf16[512,256]{1,0:T(8,128)(2,1)S(1)} %bitcast.14), custom_call_target="tpu_custom_call" | custom-call | flops 2952790016 | bytes 2883584 | tf_op jit(solution)/shard_map/residual/pallas_call | solution.py:250
  63.7 6.2 %all-to-all-start.1 = ((bf16[32,88,256]{2,1,0:T(8,128)(2,1)}), bf16[32,88,256]{2,1,0:T(8,128)(2,1)S(1)}, u32[]{:S(2)}, u32[]{:S(2)}) async-start(bf16[32,88,256]{2,1,0:T(8,128)(2,1)} %bitcast.8), calls=%async_computation.1 | async-start | bytes 2883584 | tf_op jit(solution)/shard_map/all_to_all | solution.py:383
  69.9 0.0 copy-start
  69.9 2.6 %copy-done = bf16[1,2,512,2816]{3,2,1,0:T(8,128)(2,1)S(1)} copy-done((bf16[1,2,512,2816]{3,2,1,0:T(8,128)(2,1)S(1)}, bf16[1,2,512,2816]{3,2,1,0:T(8,128)(2,1)}, u32[]{:S(2)}) %copy-start) | copy-done | bytes 5767192
  72.5 7.0 %slot_cols.1.factor = bf16[2,512,2816]{2,1,0:T(8,128)(2,1)S(1)} custom-call(s32[32,32]{1,0:T(8,128)S(1)} %bitcast.17, bf16[2,512,2816]{2,1,0:T(8,128)(2,1)S(1)} %bitcast.11, f32[1,2816]{1,0:T(1,128)S(1)} %bitcast.19), custom_call_target="tpu_custom_call" | custom-call | flops 2214592512 | bytes 11534336 | tf_op jit(solution)/shard_map/slot_cols/pallas_call | solution.py:173
  79.5 2.5 %copy-done.1 = bf16[2,512,2816]{2,1,0:T(8,128)(2,1)} copy-done((bf16[2,512,2816]{2,1,0:T(8,128)(2,1)}, bf16[2,512,2816]{2,1,0:T(8,128)(2,1)S(1)}, u32[]{:S(2)}) %copy-start.1) | copy-done | bytes 5767192
  82.0 10.8 %all-to-all-done.1 = bf16[32,88,256]{2,1,0:T(8,128)(2,1)S(1)} async-done(((bf16[32,88,256]{2,1,0:T(8,128)(2,1)}), bf16[32,88,256]{2,1,0:T(8,128)(2,1)S(1)}, u32[]{:S(2)}, u32[]{:S(2)}) %all-to-all-start.1) | async-done | bytes 1441824 | tf_op jit(solution)/shard_map/all_to_all | solution.py:383
  92.8 3.8 %gradient.1 = bf16[8,32,512]{2,1,0:T(8,128)(2,1)S(1)} custom-call(bf16[2816,256]{1,0:T(8,128)(2,1)S(1)} %bitcast.13, bf16[2,512,2816]{2,1,0:T(8,128)(2,1)} %copy-done.1), custom_call_target="tpu_custom_call" | custom-call | flops 1476395008 | bytes 1441792 | tf_op jit(solution)/shard_map/gradient/pallas_call | solution.py:302
  96.6 10.7 %all_to_all.15.arrived = bf16[8,32,512]{2,1,0:T(8,128)(2,1)S(1)} all-to-all(bf16[8,32,512]{2,1,0:T(8,128)(2,1)S(1)} %gradient.1), channel_id=1, replica_groups=mesh['freq'=8,'tile'=32] {'freq'}, dimensions={0} | all-to-all | bytes 524288 | tf_op jit(solution)/shard_map/all_to_all | solution.py:385
  107.3 0.0 copy-done.5
  107.3 2.8 %to_time.1 = bf16[512,16,128]{2,1,0:T(8,128)(2,1)} custom-call(s32[512]{0:T(512)S(1)} %copy-done.8, bf16[8,32,512]{2,1,0:T(8,128)(2,1)S(1)} %all_to_all.15.arrived, bf16[256,256]{1,0:T(8,128)(2,1)S(1)} %copy-done.5), custom_call_target="tpu_custom_call" | custom-call | tf_op jit(solution)/shard_map/to_time/pallas_call | solution.py:353
  (9 shorter events, 0.0 us)
Async XLA Ops:
  0.0 35.0 %copy-start.6 = (s32[1,32,32]{2,1,0:T(8,128)S(1)}, s32[1,32,32]{2,1,0:T(8,128)}, u32[]{:S(2)}) copy-start(s32[1,32,32]{2,1,0:T(8,128)} %param.15) | copy-start | bytes 12292
  0.0 35.0 %copy-start.10 = (f32[1,1,2816]{2,1,0:T(1,128)S(1)}, f32[1,1,2816]{2,1,0:T(1,128)}, u32[]{:S(2)}) copy-start(f32[1,1,2816]{2,1,0:T(1,128)} %param.12) | copy-start | bytes 33796
  22.8 33.0 %copy-start.4 = (bf16[1,512,256]{2,1,0:T(8,128)(2,1)S(1)}, bf16[1,512,256]{2,1,0:T(8,128)(2,1)}, u32[]{:S(2)}) copy-start(bf16[1,512,256]{2,1,0:T(8,128)(2,1)} %param.10) | copy-start | bytes 786436
  22.8 33.0 %all-to-all-start = ((bf16[32,88,256]{2,1,0:T(8,128)(2,1)}), bf16[32,88,256]{2,1,0:T(8,128)(2,1)S(1)}, u32[]{:S(2)}, u32[]{:S(2)}) async-start(bf16[32,88,256]{2,1,0:T(8,128)(2,1)} %coef.1), calls=%async_computation | async-start | bytes 2883584 | tf_op jit(solution)/shard_map/all_to_all | solution.py:379
  35.0 2.6 %copy-start.9 = (bf16[1,2,512,2816]{3,2,1,0:T(8,128)(2,1)S(1)}, bf16[1,2,512,2816]{3,2,1,0:T(8,128)(2,1)}, u32[]{:S(2)}) copy-start(bf16[1,2,512,2816]{3,2,1,0:T(8,128)(2,1)} %param.11) | copy-start | bytes 17301508
  45.7 2.5 %copy-start.2 = (bf16[2,512,2816]{2,1,0:T(8,128)(2,1)}, bf16[2,512,2816]{2,1,0:T(8,128)(2,1)S(1)}, u32[]{:S(2)}) copy-start(bf16[2,512,2816]{2,1,0:T(8,128)(2,1)S(1)} %get-tuple-element.12.factor) | copy-start | bytes 17301508
  48.2 2.5 %copy-start.3 = (bf16[2816,1024]{1,0:T(8,128)(2,1)}, bf16[2816,1024]{1,0:T(8,128)(2,1)S(1)}, u32[]{:S(2)}) copy-start(bf16[2816,1024]{1,0:T(8,128)(2,1)S(1)} %get-tuple-element.13.turned) | copy-start | bytes 17301508
  55.8 14.1 %copy-start.7 = (f32[1,1,2816]{2,1,0:T(1,128)S(1)}, f32[1,1,2816]{2,1,0:T(1,128)}, u32[]{:S(2)}) copy-start(f32[1,1,2816]{2,1,0:T(1,128)} %param.14) | copy-start | bytes 33796
  63.7 29.2 %all-to-all-start.1 = ((bf16[32,88,256]{2,1,0:T(8,128)(2,1)}), bf16[32,88,256]{2,1,0:T(8,128)(2,1)S(1)}, u32[]{:S(2)}, u32[]{:S(2)}) async-start(bf16[32,88,256]{2,1,0:T(8,128)(2,1)} %bitcast.8), calls=%async_computation.1 | async-start | bytes 2883584 | tf_op jit(solution)/shard_map/all_to_all | solution.py:383
  69.9 2.6 %copy-start = (bf16[1,2,512,2816]{3,2,1,0:T(8,128)(2,1)S(1)}, bf16[1,2,512,2816]{3,2,1,0:T(8,128)(2,1)}, u32[]{:S(2)}) copy-start(bf16[1,2,512,2816]{3,2,1,0:T(8,128)(2,1)} %param.13) | copy-start | bytes 17301508
  79.5 2.5 %copy-start.1 = (bf16[2,512,2816]{2,1,0:T(8,128)(2,1)}, bf16[2,512,2816]{2,1,0:T(8,128)(2,1)S(1)}, u32[]{:S(2)}) copy-start(bf16[2,512,2816]{2,1,0:T(8,128)(2,1)S(1)} %slot_cols.1.factor) | copy-start | bytes 17301508
  82.0 25.3 %copy-start.5 = (bf16[256,256]{1,0:T(8,128)(2,1)S(1)}, bf16[256,256]{1,0:T(8,128)(2,1)}, u32[]{:S(2)}) copy-start(bf16[256,256]{1,0:T(8,128)(2,1)} %constant.2.clone.basis) | copy-start | bytes 393220
  82.0 25.3 %copy-start.8 = (s32[512]{0:T(512)S(1)}, s32[512]{0:T(512)}, u32[]{:S(2)}) copy-start(s32[512]{0:T(512)} %mute.1) | copy-start | bytes 6148
